TPU v7x, 256 devices: a whole 4x4x8 slice. The times are simulated.
256 devices in a mesh: sample: 16 (over z, core), expert: 16 (over y, x).
Axes of the slice: x: 4, y: 4, z: 8, core: 2. Of those that a mesh axis runs over, the one named last changes fastest.
Arguments:
- queries: bfloat16 [128, 16, 8192], P('expert', 'sample'), may hold values from -8 to 8
- prompt_kv: bfloat16 [128, 1024, 1024], P('expert', 'sample'), may hold values from -8 to 8
- gen_kv: bfloat16 [128, 16, 32, 1024], P('expert', 'sample'), may hold values from -4 to 4
- gen_lengths: int32 [128, 16], P('expert', 'sample'), may hold values from 1 to 32, 256 in all within a row
- out_proj: bfloat16 [8192, 4096], P(None, 'sample'), may hold values from -1 to 1
- residual: bfloat16 [128, 16, 4096], P('expert', None, 'sample'), may hold values from -160 to 160
- norm_gain: float32 [4096], P('sample'), may hold values from 0.1 to 1.9
- w_gate_up: bfloat16 [48, 4096, 3072], P('expert', 'sample'), may hold values from -0.09375 to 0.09375
- w_down: bfloat16 [48, 1536, 4096], P('expert', None, 'sample'), may hold values from -0.15625 to 0.15625
- routes: int32 [128, 16, 8], P('expert'), may hold values from 0 to 47, all different within a row; in each aligned block of 128 rows (0 to 127, 128 to 255, ..., all dimensions but the last counted through in order) at most 26 rows name the same one
- route_probs: float32 [128, 16, 8], P('expert'), may hold values from 0.1 to 1
Outputs:
- mixed: bfloat16 [128, 16, 4096], P('expert', None, 'sample')
- expert_out: bfloat16 [128, 16, 4096], P('expert', None, 'sample')
Inputs may be any that keep to these rules, and one draw needn't show every extreme that they name: `gen_lengths`: in each prompt, at least one sample has 32 generated tokens. `routes`: each row names 8 different experts. Among the 128 rows of the prompts of one index of expert, no expert is named by more than 26 rows, a bound that some block reaches.
All inputs are finite; a program needn't handle non-finite values. No bound on the sum of `gen_lengths` on one device may be relied on, other than what follows from the above.
Results may differ from a plain program's by a relative error of at most 0.028.
Values may be sent and summed in bfloat16 or wider, within the bound.
A program may use at most 128 MiB of HBM per device.

v0:
```python
import jax
import jax.numpy as jnp
from jax import lax
from jax.sharding import PartitionSpec as P

D = 4096
FF = 1536
QHEADS = 64
KVHEADS = 4
HDIM = 128
TOPK = 8
EXP_COL = 3


NEGATIVE = -1e30
EPSILON = 1e-06


def absorb(carried, scores, value_rows):
    highest = jnp.maximum(carried[0], jnp.max(scores, axis=-1))
    rescale = jnp.exp(carried[0] - highest)
    weights = jnp.exp(scores - highest[..., None])
    weight_sum = carried[1] * rescale + jnp.sum(weights, axis=-1)
    numerator = carried[2] * rescale[..., None] + jnp.einsum(
        "brhgn,bnhd->brhgd",
        weights,
        value_rows.astype(jnp.float32),
        precision=lax.Precision.HIGHEST,
    )
    return (highest, weight_sum, numerator)


def split_cache(cache):
    kv_width = KVHEADS * HDIM
    prompts_here = cache.shape[0]
    length = cache.shape[1]
    key_rows = cache[:, :, :kv_width].reshape(prompts_here, length, KVHEADS, HDIM)
    value_rows = cache[:, :, kv_width:].reshape(prompts_here, length, KVHEADS, HDIM)
    return (key_rows, value_rows)


def score_rows(query, key_rows):
    return jnp.einsum(
        "brhgd,bnhd->brhgn", query, key_rows, preferred_element_type=jnp.float32
    ) * HDIM ** (-0.5)


def empty_state(shape):
    return (
        jnp.full(shape, NEGATIVE, jnp.float32),
        jnp.zeros(shape, jnp.float32),
        jnp.zeros(shape + (HDIM,), jnp.float32),
    )


def on_device(
    queries,
    prompt_kv,
    gen_kv,
    gen_lengths,
    out_proj,
    residual,
    norm_gain,
    w_gate_up,
    w_down,
    routes,
    route_probs,
):
    prompts_here = queries.shape[0]
    groups = QHEADS // KVHEADS
    samples = lax.axis_size("sample")
    width = residual.shape[2]
    own_query = queries.reshape(prompts_here, 1, KVHEADS, groups, HDIM)
    gen_keys, gen_values = split_cache(gen_kv[:, 0])
    positions = jnp.arange(gen_kv.shape[2], dtype=jnp.int32)
    valid = (positions[None, :] < gen_lengths)[:, None, None, None, :]
    gen_scores = jnp.where(valid, score_rows(own_query, gen_keys), NEGATIVE)
    own_state = absorb(empty_state((prompts_here, 1, KVHEADS, groups)), gen_scores, gen_values)
    key_rows, value_rows = split_cache(lax.all_gather(prompt_kv, "sample", axis=1, tiled=True))
    merged = absorb(own_state, score_rows(own_query, key_rows), value_rows)
    attended = (
        (merged[2] / merged[1][..., None])
        .astype(jnp.bfloat16)
        .reshape(prompts_here, 1, QHEADS * HDIM)
    )
    projected = jnp.einsum(
        "bnq,qd->bnd",
        lax.all_gather(attended, "sample", axis=1, tiled=True),
        out_proj,
        preferred_element_type=jnp.float32,
    )
    mixed = projected.astype(jnp.bfloat16)
    stream = residual.astype(jnp.float32) + projected
    squares = lax.psum(jnp.sum(stream * stream, axis=-1), "sample")
    factor = lax.rsqrt(squares / D + EPSILON)
    row_count = prompts_here * samples
    normed = (stream * factor[..., None] * norm_gain).astype(jnp.bfloat16).reshape(row_count, width)
    owners = lax.axis_size("expert")
    experts_all = EXP_COL * owners
    capacity = 5 * prompts_here * samples * TOPK // (4 * experts_all)
    expert_ids = routes.reshape(row_count, TOPK)
    route_weight = route_probs.reshape(row_count, TOPK)
    expert_hits = jnp.sum(
        (expert_ids[:, :, None] == jnp.arange(experts_all, dtype=jnp.int32)[None, None, :]).astype(
            jnp.int32
        ),
        axis=1,
    )
    before = jnp.cumsum(expert_hits, axis=0) - expert_hits
    arrival = jnp.take_along_axis(before, expert_ids, axis=1)
    slot_index = (expert_ids * capacity + arrival).reshape(-1)
    outgoing = (
        jnp.zeros((experts_all * capacity, width), jnp.bfloat16)
        .at[slot_index]
        .set(jnp.repeat(normed, TOPK, axis=0))
    )
    outgoing = outgoing.reshape(owners, EXP_COL, capacity, width)
    partial_sums = jnp.einsum(
        "sjcd,jdf->sjcf",
        lax.all_to_all(outgoing, "expert", split_axis=0, concat_axis=0, tiled=True),
        w_gate_up,
        preferred_element_type=jnp.float32,
    )
    gate_up = lax.psum(partial_sums.astype(jnp.bfloat16), "sample").astype(jnp.float32)
    activated = (jax.nn.silu(gate_up[..., :FF]) * gate_up[..., FF:]).astype(jnp.bfloat16)
    finished = jnp.einsum(
        "sjcf,jfd->sjcd", activated, w_down, preferred_element_type=jnp.float32
    ).astype(jnp.bfloat16)
    returned = lax.all_to_all(finished, "expert", split_axis=0, concat_axis=0, tiled=True)
    picked = jnp.take(returned.reshape(experts_all * capacity, width), slot_index, axis=0).reshape(
        row_count, TOPK, width
    )
    combined = jnp.sum(picked.astype(jnp.float32) * route_weight[:, :, None], axis=1)
    expert_out = combined.astype(jnp.bfloat16).reshape(prompts_here, samples, width)
    return (mixed, expert_out)


def solution(mesh):
    placed = (
        P("expert", "sample", None),
        P("expert", "sample", None),
        P("expert", "sample", None, None),
        P("expert", "sample"),
        P(None, "sample"),
        P("expert", None, "sample"),
        P("sample"),
        P("expert", "sample", None),
        P("expert", None, "sample"),
        P("expert", None, None),
        P("expert", None, None),
    )
    return jax.shard_map(
        on_device,
        mesh=mesh,
        in_specs=placed,
        out_specs=(P("expert", None, "sample"), P("expert", None, "sample")),
        check_vma=False,
    )
```

profile of v0, /device:TPU:1, one launch (start us, length us, event | category | flops | bytes accessed | tf_op | source)
XLA Modules:
  0.0 451.1 jit_solution(12887853357959558005)
XLA Ops:
  7.2 2.9 copy.82
  10.2 0.7 iota_compare_fusion.1
  11.0 1.1 slice_bitcast_fusion
  12.0 1.2 fusion.59
  13.3 96.6 %all-gather.3.cloned.1.call-done = bf16[8,1024,1024]{2,0,1:T(8,128)(2,1)} async-done(((bf16[8,64,1024]{2,0,1:T(8,128)(2,1)}), bf16[8,1024,1024]{2,0,1:T(8,128)(2,1)}) %all-gather.3.cloned.1.call-update) | async-done | bytes 16777232 | tf_op jit(solution)/shard_map/all_gather | solution.py:79
  109.9 11.3 %fusion.58 = (bf16[8,1024,512]{2,0,1:T(8,128)(2,1)}, bf16[8,1024,512]{2,0,1:T(8,128)(2,1)}) fusion(bf16[8,1024,1024]{2,0,1:T(8,128)(2,1)} %all-gather.3.cloned.1.call-done), kind=kLoop, calls=%fused_computation.79 | loop fusion | bytes 33554432 | tf_op jit(solution)/shard_map/slice | solution.py:37
  121.2 12.3 %copy.109 = bf16[8,1024,512]{1,2,0:T(8,128)(2,1)} copy(bf16[8,1024,512]{2,0,1:T(8,128)(2,1)} %get-tuple-element.8) | data formatting | bytes 16777216
  133.5 6.0 %bitcast_reduce_fusion = (f32[8,4,16]{2,1,0:T(4,128)S(1)}, f32[8,4,1024,16]{2,3,1,0:T(8,128)}) fusion(bf16[8,1024,4,128]{1,3,2,0:T(8,128)(2,1)} %bitcast.118, bf16[8,4,16,128]{3,0,2,1:T(8,128)(2,1)S(1)} %bitcast.124), kind=kOutput, calls=%fused_computation.14 | convolution fusion | flops 135265792 | bytes 10618880 | tf_op jit(solution)/shard_map/brhgd,bnhd->brhgn/dot_general | solution.py:43
  139.5 12.2 %copy.110 = bf16[8,1024,512]{1,2,0:T(8,128)(2,1)} copy(bf16[8,1024,512]{2,0,1:T(8,128)(2,1)} %get-tuple-element.9) | data formatting | bytes 16777216
  151.7 2.2 fusion.10
  154.0 9.0 %fusion.22 = f32[8,4,128,1,16]{2,4,1,0,3:T(8,128)S(1)} fusion(bf16[8,1024,4,128]{1,3,2,0:T(8,128)(2,1)} %bitcast.117, f32[8,4,1024,16]{2,3,1,0:T(8,128)S(1)} %copy-done.1, f32[8,4,16]{2,1,0:T(4,128)S(1)} %get-tuple-element.15), kind=kOutput, calls=%fused_computation.19 | convolution fusion | flops 806354944 | bytes 10749952 | tf_op jit(solution)/shard_map/brhgn,bnhd->brhgd/dot_general | solution.py:24
  163.4 0.4 fusion.33
  163.8 0.7 reshape.292
  165.5 7.1 %gather_fusion.1 = s32[1024]{0:T(1024)S(1)} fusion(s32[128,48]{1,0:T(8,128)S(1)} %sub.53, s32[1024]{0:T(1024)S(1)} %reshape.308), kind=kCustom, calls=%fused_computation.1 | custom fusion | bytes 16384 | tf_op jit(solution)/shard_map/jit(take_along_axis)/gather | solution.py:110
  172.6 30.1 %all-gather.5.cloned.1.call-done = bf16[8,16,8192]{2,0,1:T(8,128)(2,1)} async-done(((bf16[8,1,8192]{2,0,1:T(8,128)(2,1)}), bf16[8,16,8192]{2,0,1:T(8,128)(2,1)}) %all-gather.5.cloned.1.call-update) | async-done | bytes 2097168 | tf_op jit(solution)/shard_map/all_gather | solution.py:88
  202.7 3.6 multiply_reduce_fusion.1
  206.3 23.7 %psum.14 = f32[8,16]{0,1:T(8,128)S(1)} all-reduce(f32[8,16]{0,1:T(8,128)S(1)} %get-tuple-element.21), channel_id=1, replica_groups=mesh['sample'=16,'expert'=16] {'sample'}, use_global_device_ids=true, to_apply=%region_7.8 | all-reduce | flops 128 | bytes 1024 | tf_op jit(solution)/shard_map/psum | solution.py:94
  230.1 5.8 %scatter_custom_fusion = bf16[1248,256]{1,0:T(8,128)(2,1)} fusion(s32[1024]{0:T(1024)S(1)} %bitcast.126, bf16[]{:T(256)} %constant.35.clone.1, bf16[128,256]{1,0:T(8,128)(2,1)S(1)} %bitcast.121), kind=kCustom, calls=%fused_computation.36 | custom fusion | bytes 704514 | tf_op jit(solution)/shard_map/scatter | solution.py:115
  235.9 1.3 reshape.298
  237.1 18.6 %all_to_all.10 = bf16[16,3,26,256]{3,2,1,0:T(8,128)(2,1)S(1)} all-to-all(bf16[16,3,26,256]{3,2,1,0:T(8,128)(2,1)S(1)} %reshape.298), channel_id=1, replica_groups=mesh['sample'=16,'expert'=16] {'expert'}, dimensions={0} | all-to-all | bytes 1277952 | tf_op jit(solution)/shard_map/all_to_all | solution.py:120
  255.7 7.5 %convert_bitcast_fusion = bf16[16,3,26,3072]{3,2,0,1:T(8,128)(2,1)} fusion(bf16[3,256,3072]{2,1,0:T(8,128)(2,1)} %param.18, bf16[16,3,26,256]{3,2,1,0:T(8,128)(2,1)S(1)} %all_to_all.10), kind=kOutput, calls=%fused_computation.5 | convolution fusion | flops 1966768128 | bytes 13025280 | tf_op jit(solution)/shard_map/sjcd,jdf->sjcf/dot_general | solution.py:118
  263.2 134.2 %all-reduce.2.cloned.1.call-done = bf16[16,3,26,3072]{3,2,0,1:T(8,128)(2,1)} async-done(((bf16[16,3,26,3072]{3,2,0,1:T(8,128)(2,1)}), bf16[16,3,26,3072]{3,2,0,1:T(8,128)(2,1)}) %all-reduce.2.cloned.1.call-update) | async-done | bytes 7667728 | tf_op jit(solution)/shard_map/psum | solution.py:124
  397.3 12.4 %convert_element_type.49 = f32[16,3,26,3072]{3,2,0,1:T(8,128)} convert(bf16[16,3,26,3072]{3,2,0,1:T(8,128)(2,1)} %all-reduce.2.cloned.1.call-done) | non-fusion elementwise | flops 3833856 | bytes 23003136 | tf_op jit(solution)/shard_map/convert_element_type | solution.py:124
  409.8 8.0 %fusion.17 = bf16[16,3,26,256]{3,2,0,1:T(8,128)(2,1)S(1)} fusion(bf16[3,1536,256]{2,1,0:T(8,128)(2,1)S(1)} %copy-done, f32[16,3,26,3072]{3,2,0,1:T(8,128)} %convert_element_type.49), kind=kOutput, calls=%fused_computation.18 | convolution fusion | flops 993288192 | bytes 18333696 | tf_op jit(solution)/shard_map/sjcf,jfd->sjcd/dot_general | solution.py:126
  417.8 1.0 copy.99
  418.7 6.6 %all-to-all-start.1 = ((bf16[16,3,26,256]{3,2,1,0:T(8,128)(2,1)}), bf16[16,3,26,256]{3,2,1,0:T(8,128)(2,1)}, u32[]{:S(2)}, u32[]{:S(2)}) async-start(bf16[16,3,26,256]{3,2,1,0:T(8,128)(2,1)} %copy.99), calls=%async_computation.1 | async-start | bytes 1572864 | tf_op jit(solution)/shard_map/all_to_all | solution.py:129
  425.6 0.7 copy.107
  426.3 0.6 copy.102
  427.0 10.4 %all-to-all-done.1 = bf16[16,3,26,256]{3,2,1,0:T(8,128)(2,1)} async-done(((bf16[16,3,26,256]{3,2,1,0:T(8,128)(2,1)}), bf16[16,3,26,256]{3,2,1,0:T(8,128)(2,1)}, u32[]{:S(2)}, u32[]{:S(2)}) %all-to-all-start.1) | async-done | bytes 639008 | tf_op jit(solution)/shard_map/all_to_all | solution.py:129
  437.3 1.3 reshape.299
  438.6 3.9 gather_fusion
  442.6 1.9 multiply_reduce_fusion
  (44 shorter events, 1.8 us)
Async XLA Ops:
  7.2 402.6 %copy-start = (bf16[3,1536,256]{2,1,0:T(8,128)(2,1)S(1)}, bf16[3,1536,256]{2,1,0:T(8,128)(2,1)}, u32[]{:S(2)}) copy-start(bf16[3,1536,256]{2,1,0:T(8,128)(2,1)} %param.19) | copy-start | bytes 7077892
  7.2 102.7 %all-gather.3.cloned.1.call-start = ((), (), s32[]{:S(2)}) async-start(), calls=%async_computation.2 | async-start | bytes 17825792 | tf_op jit(solution)/shard_map/all_gather | solution.py:79
  10.2 192.5 %all-gather.5.cloned.1.call-start = ((), (), s32[]{:S(2)}) async-start(), calls=%async_computation.3 | async-start | bytes 2228224 | tf_op jit(solution)/shard_map/all_gather | solution.py:88
  121.2 12.3 %copy-start.3 = (bf16[8,1,8192]{2,0,1:T(8,128)(2,1)S(1)}, bf16[8,1,8192]{2,0,1:T(8,128)(2,1)}, u32[]{:S(2)}) copy-start(bf16[8,1,8192]{2,0,1:T(8,128)(2,1)} %param.11) | copy-start | bytes 393220
  151.7 2.3 copy-start.1
  154.0 10.6 %copy-start.4 = (s32[8,16,8]{1,2,0:T(8,128)S(1)}, s32[8,16,8]{1,2,0:T(8,128)}, u32[]{:S(2)}) copy-start(s32[8,16,8]{1,2,0:T(8,128)} %param.20) | copy-start | bytes 12292
  164.5 232.8 %all-reduce.2.cloned.1.call-start = ((), (), s32[]{:S(2)}) async-start(), calls=%async_computation.4 | async-start | bytes 18874368 | tf_op jit(solution)/shard_map/psum | solution.py:124
  165.5 37.2 %copy-start.2 = (bf16[8,16,256]{2,1,0:T(8,128)(2,1)S(1)}, bf16[8,16,256]{2,1,0:T(8,128)(2,1)}, u32[]{:S(2)}) copy-start(bf16[8,16,256]{2,1,0:T(8,128)(2,1)} %param.16) | copy-start | bytes 196612
  172.6 57.4 %copy-start.6 = (f32[256]{0:T(256)S(1)}, f32[256]{0:T(256)}, u32[]{:S(2)}) copy-start(f32[256]{0:T(256)} %param.17) | copy-start | bytes 3076
  409.8 15.8 %copy-start.5 = (f32[8,16,8]{1,2,0:T(8,128)S(1)}, f32[8,16,8]{1,2,0:T(8,128)}, u32[]{:S(2)}) copy-start(f32[8,16,8]{1,2,0:T(8,128)} %param.21) | copy-start | bytes 12292
  418.7 18.6 %all-to-all-start.1 = ((bf16[16,3,26,256]{3,2,1,0:T(8,128)(2,1)}), bf16[16,3,26,256]{3,2,1,0:T(8,128)(2,1)}, u32[]{:S(2)}, u32[]{:S(2)}) async-start(bf16[16,3,26,256]{3,2,1,0:T(8,128)(2,1)} %copy.99), calls=%async_computation.1 | async-start | bytes 1572864 | tf_op jit(solution)/shard_map/all_to_all | solution.py:129
Sparse Core Ops, SparseCore 0:
  10.3 99.5 all-gather.2
  164.7 37.9 all-gather.4
  263.3 134.0 all-reduce.1
where the time goes:
time: 453 us; the launch traced here: 451 us
  waiting for transfers between devices  271 us (60%)
  local copies, waits for them, and re-layouts  63.1 us (14%)
  blocking collectives  42.2 us (9%)
  matrix products  35.7 us (8%)
  other arithmetic  18.1 us (4%)
  between operations  14 us (3%)
  starting transfers between devices  6.7 us (1%)
    psum x1, waiting for transfers between devices, on_device(): lax.psum(partial_sums.astype(jnp.bfloat16), 'sample').astype(jnp.float32)  134 us
    all_gather x1, waiting for transfers between devices, on_device(): lax.all_gather(prompt_kv, 'sample', axis=1, tiled=True)  96.6 us
    all_gather x1, waiting for transfers between devices, on_device(): lax.all_gather(attended, 'sample', axis=1, tiled=True)  30.1 us
    unnamed x21, local copies, waits for them, and re-layouts  29.3 us
    psum x1, blocking collectives, on_device(): squares = lax.psum(jnp.sum(stream * stream, axis=-1), 'sample')  23.7 us
    all_to_all x1, blocking collectives, on_device(): lax.all_to_all(outgoing, 'expert', split_axis=0, concat_axis=0, tiled=True)  18.6 us
    convert_element_type x1, other arithmetic, on_device(): lax.psum(partial_sums.astype(jnp.bfloat16), 'sample').astype(jnp.float32)  12.4 us
    slice x1, local copies, waits for them, and re-layouts, split_cache(): cache[:, :, :kv_width].reshape(prompts_here, length, KVHEADS, HDIM)  11.3 us
  transfers between devices with their start and end apart: 4, of which 4 were waited for; matrix products, arithmetic and copies ran while one was open for 3% of the time, Pallas kernels for 0%

commit v1 on v0

v1 whole, which is shorter than its diff:
```python
import functools

import jax
import jax.numpy as jnp
from jax import lax
from jax.experimental import pallas as pl
from jax.experimental.pallas import tpu as pltpu
from jax.sharding import PartitionSpec as P

MESH = pl.DeviceIdType.MESH
HDIM = 128
GROUPS = 16
HEADS_HERE = 2
EXP_COL = 3
CAP = 26
TILE = 16
NEGATIVE = -1e30
EPSILON = 1e-06
F32 = jnp.float32
BF16 = jnp.bfloat16


def remote(src, dst, send, recv, device):
    return pltpu.make_async_remote_copy(
        src_ref=src, dst_ref=dst, send_sem=send, recv_sem=recv, device_id=device, device_id_type=MESH
    )


def greet(groups):
    barrier = pltpu.get_barrier_semaphore()
    total = 0
    for axis, size in groups:
        me = lax.axis_index(axis)

        def signal(o, carry, axis=axis, size=size, me=me):
            pl.semaphore_signal(
                barrier, inc=1, device_id={axis: lax.rem(me + o, size)}, device_id_type=MESH
            )
            return carry

        lax.fori_loop(1, size, signal, 0)
        total += size - 1
    pl.semaphore_wait(barrier, total)


def attend_kernel(
    n, q, kv, gkv, wo, res, gain, mixed, normed,
    rq, rk, rv, rgk, rgv, wov, obuf, att, sqs, sqr,
    lsem, ssem, rsem, ag_s, ag_r, sib_s, sib_r, own_sem, sq_ss, sq_rs,
):
    chips = n // 2
    half = chips // 2
    me = lax.axis_index("sample")
    z, c = me // 2, lax.rem(me, 2)
    wide = HEADS_HERE * HDIM
    values_at = 2 * wide

    def pieces(p, hp, slot):
        return (
            (q.at[p, hp], rq.at[slot]),
            (kv.at[p, :, pl.ds(hp * wide, wide)], rk.at[slot]),
            (kv.at[p, :, pl.ds(values_at + hp * wide, wide)], rv.at[slot]),
            (gkv.at[p, :, pl.ds(hp * wide, wide)], rgk.at[slot]),
            (gkv.at[p, :, pl.ds(values_at + hp * wide, wide)], rgv.at[slot]),
        )

    greet((("sample", n),))
    order = sorted(range(1, chips), key=lambda d: -min(d, chips - d))
    sent = []
    for dz in order:
        p = lax.rem(z + dz, chips)
        for hp in range(2):
            for k, (src, dst) in enumerate(pieces(p, hp, me)):
                copy = remote(src, dst, ssem.at[k, 2 * dz + hp], rsem.at[k, me], {"sample": 2 * p + hp})
                copy.start()
                sent.append(copy)
    other = 1 - c
    dyn = pl.multiple_of(other * wide, wide)
    mine = pl.multiple_of(c * wide, wide)

    def pieces_dyn(hp, off, slot):
        return (
            (q.at[z, hp], rq.at[slot]),
            (kv.at[z, :, pl.ds(off, wide)], rk.at[slot]),
            (kv.at[z, :, pl.ds(pl.multiple_of(values_at + off, wide), wide)], rv.at[slot]),
            (gkv.at[z, :, pl.ds(off, wide)], rgk.at[slot]),
            (gkv.at[z, :, pl.ds(pl.multiple_of(values_at + off, wide), wide)], rgv.at[slot]),
        )

    for k, (src, dst) in enumerate(pieces_dyn(other, dyn, me)):
        copy = remote(src, dst, ssem.at[k, 0], rsem.at[k, me], {"sample": 2 * z + other})
        copy.start()
        sent.append(copy)
    local = []
    for k, (src, dst) in enumerate(pieces_dyn(c, mine, me)):
        copy = pltpu.make_async_copy(src, dst, lsem.at[k])
        copy.start()
        local.append(copy)
    weights = pltpu.make_async_copy(wo, wov, lsem.at[5])
    weights.start()
    for copy in local:
        copy.wait()

    def arrive(o, carry):
        src = lax.rem(me + o, n)
        for k, (a, b) in enumerate(pieces(0, 0, src)):
            remote(a, b, ssem.at[k, 1], rsem.at[k, src], {"sample": src}).wait_recv()
        return carry

    lax.fori_loop(1, n, arrive, 0)

    tokens = rk.shape[0] * rk.shape[1]
    gen = rgk.shape[1]
    block = 4
    scale = HDIM ** (-0.5)
    contract = (((1,), (1,)), ((), ()))
    for h in range(HEADS_HERE):
        lanes = slice(h * HDIM, (h + 1) * HDIM)

        def attend(i, carry, h=h, lanes=lanes):
            own = pl.ds(i * block, block)
            query = rq[own, h * GROUPS:(h + 1) * GROUPS, :].reshape(block * GROUPS, HDIM)
            length = rq[own, 2 * GROUPS:3 * GROUPS, :].reshape(block * GROUPS, HDIM).astype(F32)[:, 0:1]
            keys = rk[:, :, lanes].reshape(tokens, HDIM)
            vals = rv[:, :, lanes].reshape(tokens, HDIM)
            gkeys = rgk[own, :, lanes].reshape(block * gen, HDIM)
            gvals = rgv[own, :, lanes].reshape(block * gen, HDIM)
            scores = lax.dot_general(query, keys, contract, preferred_element_type=F32) * scale
            gscores = lax.dot_general(query, gkeys, contract, preferred_element_type=F32) * scale
            row = lax.broadcasted_iota(jnp.int32, gscores.shape, 0) // GROUPS
            col = lax.broadcasted_iota(jnp.int32, gscores.shape, 1)
            place = (col - row * gen).astype(F32)
            valid = jnp.logical_and(place >= 0.0, place < length)
            gscores = jnp.where(valid, gscores, NEGATIVE)
            highest = jnp.maximum(
                jnp.max(scores, axis=1, keepdims=True), jnp.max(gscores, axis=1, keepdims=True)
            )
            weight = jnp.exp(scores - highest)
            gweight = jnp.exp(gscores - highest)
            total = jnp.sum(weight, axis=1, keepdims=True) + jnp.sum(gweight, axis=1, keepdims=True)
            out = jnp.dot(weight.astype(BF16), vals, preferred_element_type=F32)
            out = out + jnp.dot(gweight.astype(BF16), gvals, preferred_element_type=F32)
            rows = pl.ds(pl.multiple_of(i * block * GROUPS, block * GROUPS), block * GROUPS)
            obuf[h, rows, :] = (out / total).astype(BF16)
            return carry

        lax.fori_loop(0, n // block, attend, 0)

    count = n * GROUPS
    r = lax.broadcasted_iota(jnp.int32, (count, count), 0)
    k = lax.broadcasted_iota(jnp.int32, (count, count), 1)
    swap = (k == (lax.rem(r, n) * GROUPS + r // n)).astype(F32).astype(BF16)
    at = pl.ds(pl.multiple_of(z * n, n), n)
    for h in range(HEADS_HERE):
        swapped = jnp.dot(swap, obuf[h], preferred_element_type=F32).astype(BF16)
        for g in range(GROUPS):
            first = (h * GROUPS + g) * HDIM
            att[c, at, first:first + HDIM] = swapped[g * n:(g + 1) * n, :]

    width = HEADS_HERE * GROUPS * HDIM
    cut = width // 2
    right = {"sample": 2 * lax.rem(z + 1, chips) + c}
    left = {"sample": 2 * lax.rem(z + chips - 1, chips) + c}
    ways = (right, left)
    sibling = {"sample": 2 * z + other}

    def part(core, b, u):
        return att.at[core, pl.ds(pl.multiple_of(b * n, n), n), u * cut:(u + 1) * cut]

    def goes(t, d, u):
        return t < half - 1 or (t == half - 1 and u == d)

    def start(copy):
        copy.start()
        sent.append(copy)

    for u in range(2):
        for d in range(2):
            if goes(0, d, u):
                start(remote(part(c, z, u), part(c, z, u), ag_s.at[d, 0, u], ag_r.at[d, 0, u], ways[d]))
    whole = att.at[c, at, :]
    start(remote(whole, whole, own_sem.at[0], own_sem.at[1], sibling))
    for t in range(half):
        for u in range(2):
            for d in range(2):
                if not goes(t, d, u):
                    continue
                b = lax.rem(z + (chips - 1 - t if d == 0 else 1 + t), chips)
                got = part(c, b, u)
                remote(got, got, ag_s.at[d, t, u], ag_r.at[d, t, u], ways[d]).wait_recv()
                if goes(t + 1, d, u):
                    start(remote(got, got, ag_s.at[d, t + 1, u], ag_r.at[d, t + 1, u], ways[d]))
                start(remote(got, got, sib_s.at[d, t, u], sib_r.at[d, t, u], sibling))
    theirs = att.at[other, at, :]
    remote(theirs, theirs, own_sem.at[0], own_sem.at[1], sibling).wait_recv()
    for t in range(half):
        for u in range(2):
            for d in range(2):
                if goes(t, d, u):
                    b = lax.rem(z + (chips - 1 - t if d == 0 else 1 + t), chips)
                    got = part(other, b, u)
                    remote(got, got, sib_s.at[d, t, u], sib_r.at[d, t, u], sibling).wait_recv()
    weights.wait()
    rows_all = res.shape[0]
    features = res.shape[1]
    step = min(1024, width)
    projected = jnp.zeros((rows_all, features), F32)
    for core in range(2):

        def project(i, acc, core=core):
            depth = pl.ds(pl.multiple_of(i * step, step), step)
            return acc + jnp.dot(att[core, :, depth], wov[core, depth, :], preferred_element_type=F32)

        projected = lax.fori_loop(0, width // step, project, projected)
    mixed[...] = projected.astype(BF16)
    stream = res[...].astype(F32) + projected
    eye = lax.broadcasted_iota(jnp.int32, (rows_all, rows_all), 0) == lax.broadcasted_iota(
        jnp.int32, (rows_all, rows_all), 1
    )
    column = jnp.sum(stream * stream, axis=1, keepdims=True)
    across = jnp.sum(jnp.where(eye, column, 0.0), axis=0, keepdims=True)
    sqs[...] = jnp.broadcast_to(across, sqs.shape)
    for o in range(1, n):
        to = lax.rem(me + o, n)
        start(remote(sqs, sqr.at[o], sq_ss.at[o], sq_rs.at[o], {"sample": to}))
    squares = sqs[...]
    for o in range(1, n):
        remote(sqs, sqr.at[o], sq_ss.at[o], sq_rs.at[o], {"sample": lax.rem(me + n - o, n)}).wait_recv()
        squares = squares + sqr[o]
    factor = lax.rsqrt(squares / (features * n) + EPSILON)
    down = jnp.sum(jnp.where(eye, factor[0:1, :], 0.0), axis=1, keepdims=True)
    normed[...] = (stream * down * gain[...]).astype(BF16)
    for copy in sent:
        copy.wait_send()


def spans():
    out = []
    for j in range(EXP_COL):
        low = CAP * j // TILE * TILE
        high = -(-CAP * (j + 1) // TILE) * TILE
        out.append((low, high))
    return out


def expert_kernel(
    n, e, x, pick, chi, clo, wgu, wdn, out,
    xs, xr, xm0, xm1, xm2, wg, wd, pown, psib, rsib, rr, act, osend, oret,
    lsem, x_s, x_r, sib_s, sib_r, rs_s, rs_r, ag_s, ag_r, fw_s, fw_r, me_sem, o_s, o_r,
):
    chips = n // 2
    half = chips // 2
    each = e // chips
    me = lax.axis_index("sample")
    z, c = me // 2, lax.rem(me, 2)
    other = 1 - c
    col = lax.axis_index("expert")
    shift = each * (col // each)
    unit = xs.shape[1]
    quarter = pown.shape[3] // 2
    ff = 4 * quarter
    features = x.shape[1]
    right = {"sample": 2 * lax.rem(z + 1, chips) + c}
    left = {"sample": 2 * lax.rem(z + chips - 1, chips) + c}
    ways = (right, left)
    sibling = {"sample": 2 * z + other}
    xm = (xm0, xm1, xm2)

    w1 = pltpu.make_async_copy(wgu, wg, lsem.at[0])
    w1.start()
    w2 = pltpu.make_async_copy(wdn, wd, lsem.at[1])
    w2.start()
    greet((("sample", n), ("expert", e)))
    sent = []

    def start(copy):
        copy.start()
        sent.append(copy)

    chosen = jnp.dot(pick[...], x[...], preferred_element_type=F32).astype(BF16)
    xs[...] = chosen.reshape(e, unit, features)
    for o in range(1, e):
        to = lax.rem(col + o, e)
        slot = lax.rem(col + e - each * (to // each), e)
        start(remote(xs.at[to], xr.at[slot], x_s.at[o], x_r.at[o], {"expert": to}))
    xr[lax.rem(col + e - shift, e)] = xs[col]
    for o in range(1, e):
        src = lax.rem(col + e - o, e)
        slot = lax.rem(src + e - shift, e)
        remote(xs.at[0], xr.at[slot], x_s.at[o], x_r.at[o], {"expert": src}).wait_recv()

    for j, (low, high) in enumerate(spans()):
        rows = lax.broadcasted_iota(jnp.int32, (1, high - low, features), 1) + low
        keep = jnp.logical_and(rows >= CAP * j, rows < CAP * (j + 1))
        xm[j][...] = jnp.where(keep, xr[:, low:high, :].astype(F32), 0.0).astype(BF16)
    w1.wait()
    group = min(4, e)

    def partial(gq, dst, d):
        for side in range(2):
            lanes = pl.ds(pl.multiple_of(side * ff + gq * quarter, 128), quarter)

            def body(i, carry):
                own = pl.ds(i * group, group)
                tiles = {}
                for j, (low, high) in enumerate(spans()):
                    left_side = xm[j][own].reshape(group * (high - low), features)
                    y = jnp.dot(left_side, wg[j, :, lanes], preferred_element_type=F32)
                    y = y.reshape(group, high - low, quarter)
                    for tile in range(low // TILE, high // TILE):
                        piece = y[:, tile * TILE - low:(tile + 1) * TILE - low, :]
                        tiles[tile] = piece if tile not in tiles else tiles[tile] + piece
                for tile, value in tiles.items():
                    dst[d, own, tile * TILE:(tile + 1) * TILE, side * quarter:(side + 1) * quarter] = (
                        value.astype(BF16)
                    )
                return carry

            lax.fori_loop(0, e // group, body, 0)

    def chunk(d, t):
        return lax.rem(z + (chips + chips - 1 - t if d == 0 else 1 + t), chips)

    def blocks(ref, d, k):
        return ref.at[d, pl.ds(k * each, each)]

    for d in range(2):
        partial(2 * other + d, psib, d)
        for t in range(chips):
            k = chunk(d, t)
            start(remote(blocks(psib, d, k), blocks(rsib, d, k), sib_s.at[d, t], sib_r.at[d, t], sibling))

    def sib_wait(d, t):
        k = chunk(d, t)
        remote(blocks(psib, d, k), blocks(rsib, d, k), sib_s.at[d, t], sib_r.at[d, t], sibling).wait_recv()

    def hop(d, t, u):
        b = chunk(d, t) * each + u
        return remote(pown.at[d, b], rr.at[d, t, u], rs_s.at[d, t, u], rs_r.at[d, t, u], ways[d])

    for d in range(2):
        partial(2 * c + d, pown, d)
        sib_wait(d, 0)
        for u in range(each):
            b = chunk(d, 0) * each + u
            pown[d, b] = (pown[d, b].astype(F32) + rsib[d, b].astype(F32)).astype(BF16)
            hop(d, 0, u).start()

    def ring(t, carry):
        for d in range(2):
            sib_wait(d, t)
        for u in range(each):
            for d in range(2):
                b = chunk(d, t) * each + u
                hop(d, t - 1, u).wait_recv()
                value = pown[d, b].astype(F32) + rsib[d, b].astype(F32) + rr[d, t - 1, u].astype(F32)
                pown[d, b] = value.astype(BF16)
                hop(d, t, u).start()
        return carry

    lax.fori_loop(1, chips - 1, ring, 0)
    for d in range(2):
        sib_wait(d, chips - 1)
    for u in range(each):
        b = z * each + u
        for d in range(2):
            hop(d, chips - 2, u).wait_recv()
            value = pown[d, b].astype(F32) + rsib[d, b].astype(F32) + rr[d, chips - 2, u].astype(F32)
            gate = value[:, :quarter]
            act[c, b, :, d * quarter:(d + 1) * quarter] = (
                gate / (1.0 + jnp.exp(-gate)) * value[:, quarter:]
            ).astype(BF16)

    def goes(t, d, u):
        return t < half - 1 or (t == half - 1 and u % 2 == d)

    def spread(d, t, u, b):
        return remote(act.at[c, b], act.at[c, b], ag_s.at[d, t, u], ag_r.at[d, t, u], ways[d])

    def hand(core, sem, b):
        return remote(act.at[core, b], act.at[core, b], fw_s.at[sem], fw_r.at[sem], sibling)

    def code(d, t, u):
        return (t * 2 + d) * each + u

    for u in range(each):
        b = z * each + u
        for d in range(2):
            if goes(0, d, u):
                start(spread(d, 0, u, b))
        mine = remote(act.at[c, b], act.at[c, b], me_sem.at[0, u], me_sem.at[1, u], sibling)
        start(mine)
    w2.wait()

    def finish(slots):
        pieces = [None] * (unit // TILE)
        count = len(slots)
        for j, (low, high) in enumerate(spans()):
            tall = high - low
            y = None
            for core in range(2):
                lhs = jnp.concatenate([act[core, b, low:high, :] for b in slots], axis=0)
                term = jnp.dot(
                    lhs, wd[j, core * 2 * quarter:(core + 1) * 2 * quarter, :], preferred_element_type=F32
                )
                y = term if y is None else y + term
            for tile in range(low // TILE, high // TILE):
                rows = lax.broadcasted_iota(jnp.int32, (TILE, 1), 0) + tile * TILE
                keep = jnp.logical_and(rows >= CAP * j, rows < CAP * (j + 1))
                got = []
                for i in range(count):
                    first = i * tall + tile * TILE - low
                    got.append(jnp.where(keep, y[first:first + TILE, :], 0.0))
                if pieces[tile] is None:
                    pieces[tile] = got
                else:
                    pieces[tile] = [p + g for p, g in zip(pieces[tile], got)]
        for i, b in enumerate(slots):
            for tile in range(unit // TILE):
                osend[b, tile * TILE:(tile + 1) * TILE, :] = pieces[tile][i].astype(BF16)
            target = lax.rem(b + shift, e)

            @pl.when(target != col)
            def _():
                remote(osend.at[b], oret.at[col], o_s.at[b], o_r.at[col], {"expert": target}).start()

            @pl.when(target == col)
            def _():
                oret[col] = osend[b]

    pending = []
    for u in range(each):
        b = z * each + u
        pending.append(
            (b, remote(act.at[other, b], act.at[other, b], me_sem.at[0, u], me_sem.at[1, u], sibling))
        )
    for t in range(half):
        arrived = []
        for u in range(each):
            for d in range(2):
                if not goes(t, d, u):
                    continue
                k = lax.rem(z + (chips - 1 - t if d == 0 else 1 + t), chips)
                b = k * each + u
                spread(d, t, u, b).wait_recv()
                if goes(t + 1, d, u):
                    start(spread(d, t + 1, u, b))
                start(hand(c, code(d, t, u), b))
                arrived.append((b, hand(other, code(d, t, u), b)))
        for b, copy in pending:
            copy.wait_recv()
        finish([b for b, copy in pending])
        pending = arrived
    for b, copy in pending:
        copy.wait_recv()
    finish([b for b, copy in pending])

    for o in range(1, e):
        src = lax.rem(col + o, e)
        remote(osend.at[0], oret.at[src], o_s.at[0], o_r.at[src], {"expert": src}).wait_recv()
    returned = oret[...].reshape(e * unit, out.shape[1])
    total = jnp.dot(chi[...], returned, preferred_element_type=F32)
    total = total + jnp.dot(clo[...], returned, preferred_element_type=F32)
    out[...] = total.astype(BF16)

    for copy in sent:
        copy.wait_send()

    def drain(t, carry):
        for d in range(2):
            for u in range(each):
                hop(d, t, u).wait_send()
        return carry

    lax.fori_loop(0, chips - 1, drain, 0)

    def drain_out(b, carry):
        target = lax.rem(b + shift, e)

        @pl.when(target != col)
        def _():
            remote(osend.at[b], oret.at[col], o_s.at[b], o_r.at[col], {"expert": target}).wait_send()

        return carry

    lax.fori_loop(0, e, drain_out, 0)


def on_device(
    n, e, queries, prompt_kv, gen_kv, gen_lengths, out_proj, residual, norm_gain,
    w_gate_up, w_down, routes, route_probs,
):
    prompts = queries.shape[0]
    rows = prompts * n
    features = residual.shape[2]
    chips = n // 2
    half = chips // 2
    each = e // chips
    topk = routes.shape[2]
    experts = EXP_COL * e
    unit = -(-EXP_COL * CAP // TILE) * TILE

    ids = routes.reshape(rows, topk)
    probs = route_probs.reshape(rows, topk)
    named = ids[:, :, None] == jnp.arange(experts, dtype=jnp.int32)[None, None, :]
    hits = jnp.sum(named.astype(F32), axis=1)
    weight = jnp.sum(jnp.where(named, probs[:, :, None], 0.0), axis=1)
    earlier = (jnp.arange(rows)[:, None] > jnp.arange(rows)[None, :]).astype(BF16)
    before = jnp.dot(earlier, hits.astype(BF16), preferred_element_type=F32)
    place = jnp.where(hits > 0, before, -1.0)
    slots = jnp.arange(CAP, dtype=F32)
    is_slot = place.T.reshape(e, EXP_COL, 1, rows) == slots[None, None, :, None]
    spare = ((0, 0), (0, unit - EXP_COL * CAP), (0, 0))
    pick = jnp.pad(is_slot.astype(BF16).reshape(e, EXP_COL * CAP, rows), spare).reshape(e * unit, rows)
    mix = jnp.where(
        place.reshape(rows, e, EXP_COL, 1) == slots[None, None, None, :],
        weight.reshape(rows, e, EXP_COL, 1),
        0.0,
    ).reshape(rows, e, EXP_COL * CAP)
    mix = jnp.pad(mix, ((0, 0), (0, 0), (0, unit - EXP_COL * CAP))).reshape(rows, e * unit)
    high = lax.reduce_precision(mix, 8, 7)
    chi = high.astype(BF16)
    clo = (mix - high).astype(BF16)

    heads = queries.shape[2] // HDIM
    lens = jnp.broadcast_to(gen_lengths.astype(BF16)[:, :, None, None], (prompts, 2, GROUPS, HDIM))
    q = jnp.concatenate([queries.reshape(prompts, 2, heads // 2, HDIM), lens], axis=2)
    width = HEADS_HERE * GROUPS * HDIM
    wide = HEADS_HERE * HDIM
    tokens, gen = prompt_kv.shape[1], gen_kv.shape[2]
    anywhere = pl.BlockSpec(memory_space=pl.ANY)
    vmem = pl.BlockSpec(memory_space=pltpu.VMEM)
    dma = pltpu.SemaphoreType.DMA
    mixed, normed = pl.pallas_call(
        functools.partial(attend_kernel, n),
        out_shape=(jax.ShapeDtypeStruct((rows, features), BF16), jax.ShapeDtypeStruct((rows, features), BF16)),
        in_specs=[anywhere] * 4 + [vmem] * 2,
        out_specs=(vmem, vmem),
        scratch_shapes=[
            pltpu.VMEM((n, 3 * GROUPS, HDIM), BF16),
            pltpu.VMEM((n, tokens, wide), BF16),
            pltpu.VMEM((n, tokens, wide), BF16),
            pltpu.VMEM((n, gen, wide), BF16),
            pltpu.VMEM((n, gen, wide), BF16),
            pltpu.VMEM((2, width, features), BF16),
            pltpu.VMEM((HEADS_HERE, n * GROUPS, HDIM), BF16),
            pltpu.VMEM((2, rows, width), BF16),
            pltpu.VMEM((8, rows), F32),
            pltpu.VMEM((n, 8, rows), F32),
            dma((6,)),
            dma((5, n)),
            dma((5, n)),
            dma((2, half, 2)),
            dma((2, half, 2)),
            dma((2, half, 2)),
            dma((2, half, 2)),
            dma((2,)),
            dma((n,)),
            dma((n,)),
        ],
        compiler_params=pltpu.CompilerParams(
            collective_id=0, has_side_effects=True, vmem_limit_bytes=40 << 20
        ),
        name="attend",
    )(
        q,
        prompt_kv,
        gen_kv.reshape(prompts, gen, gen_kv.shape[3]),
        out_proj.reshape(2, width, features),
        residual.reshape(rows, features),
        norm_gain.reshape(1, features),
    )

    quarter = w_gate_up.shape[2] // 8
    out_features = w_down.shape[2]
    band = spans()
    expert_out = pl.pallas_call(
        functools.partial(expert_kernel, n, e),
        out_shape=jax.ShapeDtypeStruct((rows, out_features), BF16),
        in_specs=[vmem] * 4 + [anywhere] * 2,
        out_specs=vmem,
        scratch_shapes=[
            pltpu.VMEM((e, unit, features), BF16),
            pltpu.VMEM((e, unit, features), BF16),
        ]
        + [pltpu.VMEM((e, top - low, features), BF16) for low, top in band]
        + [
            pltpu.VMEM(w_gate_up.shape, BF16),
            pltpu.VMEM(w_down.shape, BF16),
            pltpu.VMEM((2, e, unit, 2 * quarter), BF16),
            pltpu.VMEM((2, e, unit, 2 * quarter), BF16),
            pltpu.VMEM((2, e, unit, 2 * quarter), BF16),
            pltpu.VMEM((2, chips - 1, each, unit, 2 * quarter), BF16),
            pltpu.VMEM((2, e, unit, 2 * quarter), BF16),
            pltpu.VMEM((e, unit, out_features), BF16),
            pltpu.VMEM((e, unit, out_features), BF16),
            dma((2,)),
            dma((e,)),
            dma((e,)),
            dma((2, chips)),
            dma((2, chips)),
            dma((2, chips - 1, each)),
            dma((2, chips - 1, each)),
            dma((2, half, each)),
            dma((2, half, each)),
            dma((2 * half * each,)),
            dma((2 * half * each,)),
            dma((2, each)),
            dma((e,)),
            dma((e,)),
        ],
        compiler_params=pltpu.CompilerParams(
            collective_id=1, has_side_effects=True, vmem_limit_bytes=56 << 20
        ),
        name="experts",
    )(normed, pick, chi, clo, w_gate_up, w_down)
    shape = (prompts, n, features)
    return (mixed.reshape(shape), expert_out.reshape(shape))


def solution(mesh):
    placed = (
        P("expert", "sample", None),
        P("expert", "sample", None),
        P("expert", "sample", None, None),
        P("expert", "sample"),
        P(None, "sample"),
        P("expert", None, "sample"),
        P("sample"),
        P("expert", "sample", None),
        P("expert", None, "sample"),
        P("expert", None, None),
        P("expert", None, None),
    )
    return jax.shard_map(
        functools.partial(on_device, mesh.shape["sample"], mesh.shape["expert"]),
        mesh=mesh,
        in_specs=placed,
        out_specs=(P("expert", None, "sample"), P("expert", None, "sample")),
        check_vma=False,
    )
```

time: 453 us -> 187 us (0.41)
  waiting for transfers between devices: 271 us -> 0 us
  Pallas kernels: 0 us -> 176 us
  local copies, waits for them, and re-layouts: 63.1 us -> 8.22 us
  blocking collectives: 42.2 us -> 0 us
  matrix products: 35.7 us -> 0.14 us
  other arithmetic: 18.1 us -> 1.36 us
  between operations: 14 us -> 0.86 us
  starting transfers between devices: 6.7 us -> 0 us
    pallas_call x0 -> x2, Pallas kernels: none -> 176 us  [the longest x1 97.6 us: on_device(): pl.pallas_call(functools.partial(expert_kernel, n, e), out_shape=jax.Shap...]
    psum x1 -> x0, waiting for transfers between devices: 134 us -> none  [on_device(): lax.psum(partial_sums.astype(jnp.bfloat16), 'sample').astype(jnp.float32)]
    all_gather x2 -> x0, waiting for transfers between devices: 127 us -> none  [the longest x1 96.6 us: on_device(): lax.all_gather(prompt_kv, 'sample', axis=1, tiled=True)]
    dot_general x7 -> x1, matrix products: 35.7 us -> 0.14 us  [on_device(): before = jnp.dot(earlier, hits.astype(BF16), preferred_element_type=F32)]
    psum x1 -> x0, blocking collectives: 23.7 us -> none  [on_device(): squares = lax.psum(jnp.sum(stream * stream, axis=-1), 'sample')]
    unnamed x21 -> x22, local copies, waits for them, and re-layouts: 29.3 us -> 6.74 us
    all_to_all x1 -> x0, blocking collectives: 18.6 us -> none  [on_device(): lax.all_to_all(outgoing, 'expert', split_axis=0, concat_axis=0, tiled=True)]
    convert_element_type x2 -> x1, other arithmetic: 12.5 us -> 0.93 us  [on_device(): clo = (mix - high).astype(BF16)]
  transfers between devices with their start and end apart: 4 -> 0, of which waited for: 4 -> 0; matrix products, arithmetic and copies ran while one was open for 3% -> 0% of each run, Pallas kernels for 0% -> 0%
where the time goes in v1:
time: 187 us; the launch traced here: 186 us
  Pallas kernels  176 us (94%)
  local copies, waits for them, and re-layouts  8.22 us (4%)
    pallas_call x1, Pallas kernels, on_device(): pl.pallas_call(functools.partial(expert_kernel, n, e), out_shape=jax.Shap...  97.6 us
    pallas_call x1, Pallas kernels, on_device(): pl.pallas_call(functools.partial(attend_kernel, n), out_shape=(jax.ShapeD...  78.3 us
    unnamed x22, local copies, waits for them, and re-layouts  6.74 us

profile of v1, /device:TPU:1, one launch (start us, length us, event | category | flops | bytes accessed | tf_op | source)
XLA Modules:
  0.0 186.5 jit_solution(5309363917449445971)
XLA Ops:
  0.6 0.0 copy-start.6
  0.6 0.0 copy-start.7
  0.6 0.8 copy.29
  1.4 0.1 broadcast_in_dim.50
  1.5 0.8 copy.25
  2.3 0.1 eq.59
  2.4 0.0 copy-start.1
  2.4 0.0 copy-start.2
  2.4 0.0 copy-start.3
  2.5 0.0 copy-start.5
  2.5 0.1 convolution_select_fusion
  2.7 0.1 eq.67
  2.8 0.2 bitcast_select_fusion
  2.9 0.2 copy.34
  3.2 0.2 copy.32
  3.4 0.9 fusion
  4.4 0.2 bitcast_compare_fusion.1
  4.6 0.1 pad_convert_fusion
  4.6 0.8 copy.27
  5.4 0.0 copy-done.6
  5.5 0.0 copy-done.7
  5.5 0.1 broadcast_in_dim.48
  5.6 0.0 copy-done.1
  5.6 0.0 copy-done.2
  5.6 0.0 copy-start
  5.6 2.2 %copy-done = bf16[8192,256]{1,0:T(8,128)(2,1)S(1)} copy-done((bf16[8192,256]{1,0:T(8,128)(2,1)S(1)}, bf16[8192,256]{1,0:T(8,128)(2,1)}, u32[]{:S(2)}) %copy-start) | copy-done | bytes 4194328
  7.8 78.3 %attend.1 = (bf16[128,256]{1,0:T(8,128)(2,1)S(1)}, bf16[128,256]{1,0:T(8,128)(2,1)S(1)}) custom-call(bf16[8,2,48,128]{3,2,1,0:T(8,128)(2,1)S(1)} %pad_maximum_fusion.q, bf16[8,64,1024]{2,1,0:T(8,128)(2,1)S(1)} %copy-done.1, bf16[8,32,1024]{2,1,0:T(8,128)(2,1)S(1)} %bitcast.33, bf16[2,4096,256]{2,1,0:T(8,128)(2,1)S(1)} %bitcast.32, ...), custom_call_target="tpu_custom_call" | custom-call | tf_op jit(solution)/shard_map/attend/pallas_call | solution.py:534
  86.2 0.0 copy-start.4
  86.2 0.6 copy-done.4
  86.8 97.6 %experts.1 = bf16[128,256]{1,0:T(8,128)(2,1)} custom-call(bf16[128,256]{1,0:T(8,128)(2,1)} %copy-done.4, bf16[1280,128]{1,0:T(8,128)(2,1)} %bitcast.38, bf16[128,1280]{1,0:T(8,128)(2,1)} %get-tuple-element.9.chi, bf16[128,1280]{1,0:T(8,128)(2,1)} %get-tuple-element.8.clo, bf16[3,256,3072]{2,1,0:T(8,128)(2,1)} %wgu.1, bf16[3,1536,256]{2,1,0:T(8,128)(2,1)} %wdn.1), custom_call_target="tpu_custom_call" | custom-call | tf_op jit(solution)/shard_map/experts/pallas_call | solution.py:577
  184.4 0.6 copy.38
  185.0 1.5 copy.39
  (14 shorter events, 0.2 us)
Async XLA Ops:
  0.6 4.8 %copy-start.6 = (bf16[8,1,8192]{2,0,1:T(8,128)(2,1)S(1)}, bf16[8,1,8192]{2,0,1:T(8,128)(2,1)}, u32[]{:S(2)}) copy-start(bf16[8,1,8192]{2,0,1:T(8,128)(2,1)} %param.11) | copy-start | bytes 393220
  0.6 4.8 %copy-start.7 = (s32[8,1]{0,1:T(1,128)S(1)}, s32[8,1]{0,1:T(1,128)}, u32[]{:S(2)}) copy-start(s32[8,1]{0,1:T(1,128)} %param.14) | copy-start | bytes 100
  2.4 3.2 %copy-start.1 = (bf16[8,64,1024]{2,1,0:T(8,128)(2,1)S(1)}, bf16[8,64,1024]{2,1,0:T(8,128)(2,1)}, u32[]{:S(2)}) copy-start(bf16[8,64,1024]{2,1,0:T(8,128)(2,1)} %kv.1) | copy-start | bytes 3145732
  2.4 3.2 %copy-start.2 = (bf16[8,1,32,1024]{3,2,1,0:T(8,128)(2,1)S(1)}, bf16[8,1,32,1024]{3,2,1,0:T(8,128)(2,1)}, u32[]{:S(2)}) copy-start(bf16[8,1,32,1024]{3,2,1,0:T(8,128)(2,1)} %param.13) | copy-start | bytes 1572868
  2.4 3.2 %copy-start.3 = (bf16[8,16,256]{2,1,0:T(8,128)(2,1)S(1)}, bf16[8,16,256]{2,1,0:T(8,128)(2,1)}, u32[]{:S(2)}) copy-start(bf16[8,16,256]{2,1,0:T(8,128)(2,1)} %param.16) | copy-start | bytes 196612
  2.5 3.2 %copy-start.5 = (f32[256]{0:T(256)S(1)}, f32[256]{0:T(256)}, u32[]{:S(2)}) copy-start(f32[256]{0:T(256)} %param.17) | copy-start | bytes 3076
  5.6 2.2 %copy-start = (bf16[8192,256]{1,0:T(8,128)(2,1)S(1)}, bf16[8192,256]{1,0:T(8,128)(2,1)}, u32[]{:S(2)}) copy-start(bf16[8192,256]{1,0:T(8,128)(2,1)} %param.15) | copy-start | bytes 12582916
  86.2 0.6 copy-start.4

commit v2 on v0

v2 whole, which is shorter than its diff:
```python
import functools

import jax
import jax.numpy as jnp
from jax import lax
from jax.experimental import pallas as pl
from jax.experimental.pallas import tpu as pltpu
from jax.sharding import PartitionSpec as P

MESH = pl.DeviceIdType.MESH
HDIM = 128
GROUPS = 16
KVHEADS = 4
HERE = 2
EXP_COL = 3
CAP = 26
TILE = 16
PIECES = 4
NEGATIVE = -1e30
EPSILON = 1e-06
F32 = jnp.float32
BF16 = jnp.bfloat16
NT = (((1,), (1,)), ((), ()))


def remote(src, dst, send, recv, device):
    return pltpu.make_async_remote_copy(
        src_ref=src, dst_ref=dst, send_sem=send, recv_sem=recv, device_id=device, device_id_type=MESH
    )


def spans():
    out = []
    for j in range(EXP_COL):
        low = CAP * j // TILE * TILE
        high = -(-CAP * (j + 1) // TILE) * TILE
        out.append((low, high))
    return out


def merge_tile(tile, parts):
    if len(parts) == 1:
        return parts[0][1]
    (first, a), (second, b) = parts
    shape = (1,) * (a.ndim - 2) + (TILE, 1)
    rows = lax.broadcasted_iota(jnp.int32, shape, a.ndim - 2) + tile * TILE
    return jnp.where(rows < CAP * (first + 1), a, b)


def token_order(chips):
    return [0] + sorted(range(1, chips), key=lambda d: -min(d, chips - d))


def kernel(
    n, e,
    q, lens, kv, gkv, wo, res, gain, ids, probs, wgu, wdn,
    mixed, out,
    kvv, gv, gmsg, rq, rm, rk, rv, wov, wg, wd, ost, mst, lst, obuf, att, sqs, sqr,
    place, pick, chi, clo, y, xs, xr, pown, psib, rsib, rr, act, osend, oret, fsend, frecv,
    lsem, ex_s, ex_r, ag_s, ag_r, sib_s, sib_r, own_sem, sq_ss, sq_rs,
    x_s, x_r, ps_s, ps_r, rs_s, rs_r, aa_s, aa_r, fw_s, fw_r, me_sem, o_s, o_r, f_s, f_r,
):
    chips = n // 2
    half = chips // 2
    each = e // chips
    me = lax.axis_index("sample")
    col = lax.axis_index("expert")
    z, c = me // 2, lax.rem(me, 2)
    other = 1 - c
    wide = HERE * HDIM
    right = {"sample": 2 * lax.rem(z + 1, chips) + c}
    left = {"sample": 2 * lax.rem(z + chips - 1, chips) + c}
    ways = (right, left)
    sibling = {"sample": 2 * z + other}
    unit = xs.shape[1]
    rows_all, features = res.shape
    sent = []

    def start(copy):
        copy.start()
        sent.append(copy)

    def fetch(src, dst, k):
        copy = pltpu.make_async_copy(src, dst, lsem.at[k])
        copy.start()
        return copy

    fetch_g = fetch(gkv, gv, 1)
    fetch_kv = fetch(kv, kvv, 2)

    barrier = pltpu.get_barrier_semaphore()

    def greet_sample(o, carry):
        pl.semaphore_signal(barrier, inc=1, device_id={"sample": lax.rem(me + o, n)}, device_id_type=MESH)
        return carry

    def greet_expert(o, carry):
        pl.semaphore_signal(barrier, inc=1, device_id={"expert": lax.rem(col + o, e)}, device_id_type=MESH)
        return carry

    lax.fori_loop(1, n, greet_sample, 0)
    lax.fori_loop(1, e, greet_expert, 0)

    fetch_g.wait()
    prompts = q.shape[0]
    gen = gv.shape[1]
    scale = HDIM ** (-0.5)
    tall = prompts * GROUPS
    length = jnp.broadcast_to(lens[...], (prompts, GROUPS, HDIM)).reshape(tall, HDIM)[:, 0:1]
    lane = lax.broadcasted_iota(jnp.int32, (tall, HDIM), 1)
    for hp in range(2):
        stats = jnp.zeros((tall, HDIM), F32)
        for hl in range(HERE):
            h = hp * HERE + hl
            query = q[:, h * GROUPS:(h + 1) * GROUPS, :].reshape(tall, HDIM)
            keys = gv[:, :, h * HDIM:(h + 1) * HDIM].reshape(prompts * gen, HDIM)
            vals = gv[:, :, (KVHEADS + h) * HDIM:(KVHEADS + h + 1) * HDIM].reshape(prompts * gen, HDIM)
            scores = lax.dot_general(query, keys, NT, preferred_element_type=F32) * scale
            row = lax.broadcasted_iota(jnp.int32, scores.shape, 0) // GROUPS
            at_key = (lax.broadcasted_iota(jnp.int32, scores.shape, 1) - row * gen).astype(F32)
            scores = jnp.where(jnp.logical_and(at_key >= 0.0, at_key < length), scores, NEGATIVE)
            highest = jnp.max(scores, axis=1, keepdims=True)
            weight = jnp.exp(scores - highest)
            total = jnp.sum(weight, axis=1, keepdims=True)
            got = jnp.dot(weight.astype(BF16), vals, preferred_element_type=F32) / total
            gmsg[:, hp, hl * GROUPS:(hl + 1) * GROUPS, :] = got.astype(BF16).reshape(prompts, GROUPS, HDIM)
            level = highest + jnp.log(total)
            for k in range(3):
                part = level.astype(BF16).astype(F32)
                level = level - part
                stats = jnp.where(lane == 3 * hl + k, part, stats)
        gmsg[:, hp, HERE * GROUPS:, :] = stats.astype(BF16).reshape(prompts, GROUPS, HDIM)
    fetch_kv.wait()

    pl.semaphore_wait(barrier, n - 1 + e - 1)

    order = token_order(chips)
    where_of = {d: i for i, d in enumerate(order)}

    def q_pair(p, hp):
        return q.at[p, pl.ds(pl.multiple_of(hp * HERE * GROUPS, HERE * GROUPS), HERE * GROUPS)], rq.at[me]

    def m_pair(p, hp):
        return gmsg.at[p, hp], rm.at[me]

    def k_pair(p, hp, slot):
        return kvv.at[p, :, pl.ds(pl.multiple_of(hp * wide, wide), wide)], rk.at[slot]

    def v_pair(p, hp, slot):
        return kvv.at[p, :, pl.ds(pl.multiple_of((2 + hp) * wide, wide), wide)], rv.at[slot]

    def exchange(kind, dz, hp):
        p = lax.rem(z + dz, chips)
        slot = 2 * where_of[(chips - dz) % chips] + c
        src, dst = (
            q_pair(p, hp), m_pair(p, hp), k_pair(p, hp, slot), v_pair(p, hp, slot)
        )[kind]
        target = {"sample": 2 * p + hp}
        start(remote(src, dst, ex_s.at[kind, 2 * dz + (hp if dz else 0)], ex_r.at[kind, slot], target))

    for kind in range(2):
        for dz in order[1:]:
            for hp in range(2):
                exchange(kind, dz, hp)
        exchange(kind, 0, other)
    exchange(2, 0, other)
    exchange(3, 0, other)
    for dz in order[1:]:
        for hp in range(2):
            exchange(2, dz, hp)
            exchange(3, dz, hp)
    local = []
    for kind, (src, dst) in enumerate((q_pair(z, c), m_pair(z, c), k_pair(z, c, c), v_pair(z, c, c))):
        local.append(fetch(src, dst, kind))
    fetch_wo = fetch(wo, wov, 4)
    fetch_wg = fetch(wgu, wg, 5)
    fetch_wd = fetch(wdn, wd, 6)

    experts = place.shape[1]
    topk = ids.shape[1]
    named = jnp.zeros((topk, rows_all), F32)
    given = jnp.zeros((topk, rows_all), F32)
    for p in range(prompts):
        sample = lax.broadcasted_iota(jnp.int32, (n, rows_all), 0)
        there = lax.broadcasted_iota(jnp.int32, (n, rows_all), 1) == sample + p * n
        there = jnp.where(there, 1.0, 0.0).astype(BF16)
        named = named + jnp.dot(ids[p].astype(F32).astype(BF16), there, preferred_element_type=F32)
        rest = probs[p]
        for k in range(3):
            part = rest.astype(BF16)
            rest = rest - part.astype(F32)
            given = given + jnp.dot(part, there, preferred_element_type=F32)
    lane = lax.broadcasted_iota(jnp.int32, (rows_all, experts), 1)
    expert_row = lax.broadcasted_iota(jnp.int32, (experts, rows_all), 0).astype(F32)
    hits = jnp.zeros((experts, rows_all), F32)
    share_t = jnp.zeros((experts, rows_all), F32)
    for k in range(topk):
        same = expert_row == named[k:k + 1, :]
        hits = hits + jnp.where(same, 1.0, 0.0)
        share_t = share_t + jnp.where(same, given[k:k + 1, :], 0.0)
    square = (rows_all, rows_all)
    row_index = lax.broadcasted_iota(jnp.int32, square, 0)
    lane_index = lax.broadcasted_iota(jnp.int32, square, 1)
    above = jnp.where(row_index < lane_index, 1.0, 0.0).astype(BF16)
    eye_bf = jnp.where(row_index == lane_index, 1.0, 0.0).astype(BF16)
    before = jnp.dot(hits.astype(BF16), above, preferred_element_type=F32)
    place_t = jnp.where(hits > 0.5, before, -1.0).astype(BF16)
    place[...] = lax.dot_general(eye_bf, place_t, NT, preferred_element_type=F32).astype(BF16)
    at = lax.broadcasted_iota(jnp.int32, (e, unit, experts), 1)
    local_expert = jnp.zeros((e, unit, experts), jnp.int32)
    for j in range(1, EXP_COL):
        local_expert = local_expert + jnp.where(at >= CAP * j, 1, 0)
    slot_of = (at - CAP * local_expert).astype(F32)
    owner = lax.broadcasted_iota(jnp.int32, (e, unit, experts), 0) * EXP_COL + local_expert
    on_lane = lax.broadcasted_iota(jnp.int32, (e, unit, experts), 2)
    table = jnp.where(owner == on_lane, 1.0, 0.0).astype(BF16).reshape(e * unit, experts)
    seen = jnp.dot(table, place_t, preferred_element_type=F32)
    pick[...] = jnp.where(seen.reshape(e, unit, rows_all) == slot_of[:, :, :rows_all], 1.0, 0.0).astype(BF16)
    slot_table = jnp.where(on_lane == 0, slot_of, 0.0).astype(BF16).reshape(e * unit, experts)
    first_lane = jnp.where(lane == 0, 1.0, 0.0).astype(BF16)
    slot_row = lax.dot_general(first_lane, slot_table, NT, preferred_element_type=F32)
    placed = lax.dot_general(place[...], table, NT, preferred_element_type=F32)
    chosen = placed == slot_row
    for k, ref in enumerate((chi, clo)):
        part_t = share_t.astype(BF16)
        share_t = share_t - part_t.astype(F32)
        part = lax.dot_general(eye_bf, part_t, NT, preferred_element_type=F32).astype(BF16)
        spread_part = lax.dot_general(part, table, NT, preferred_element_type=F32)
        ref[...] = jnp.where(chosen, spread_part, 0.0).astype(BF16)

    for copy in local:
        copy.wait()

    def arrived(kind, slot):
        if kind == 0:
            src, dst = q_pair(0, 0)
        elif kind == 1:
            src, dst = m_pair(0, 0)
        elif kind == 2:
            src, dst = k_pair(0, 0, slot)
        else:
            src, dst = v_pair(0, 0, slot)
        remote(src, dst, ex_s.at[kind, 1], ex_r.at[kind, slot], sibling).wait_recv()

    def arrive_all(kinds, low, high):
        def body(i, carry):
            for kind in kinds:
                arrived(kind, i)
            return carry

        lax.fori_loop(low, high, body, 0)

    for kind in range(4):
        arrived(kind, other)
    arrive_all((0, 1), 2, n)
    first = n // 2
    arrive_all((2, 3), 2, first)
    block = min(8, n)
    slab = block * GROUPS

    def absorb(h, i, low, high, highest, total, acc):
        own = pl.ds(i * block, block)
        query = rq[own, h * GROUPS:(h + 1) * GROUPS, :].reshape(slab, HDIM)
        lanes = slice(h * HDIM, (h + 1) * HDIM)
        count = (high - low) * rk.shape[1]
        keys = rk[low:high, :, lanes].reshape(count, HDIM)
        vals = rv[low:high, :, lanes].reshape(count, HDIM)
        scores = lax.dot_general(query, keys, NT, preferred_element_type=F32) * scale
        peak = jnp.maximum(highest, jnp.max(scores, axis=1, keepdims=True))
        kept = jnp.exp(highest - peak)
        weight = jnp.exp(scores - peak)
        total = total * kept + jnp.sum(weight, axis=1, keepdims=True)
        acc = acc * kept + jnp.dot(weight.astype(BF16), vals, preferred_element_type=F32)
        return peak, total, acc

    def slab_rows(i):
        return pl.ds(pl.multiple_of(i * slab, slab), slab)

    for h in range(HERE):

        def stage_one(i, carry, h=h):
            own = pl.ds(i * block, block)
            stats = rm[own, HERE * GROUPS:, :].reshape(slab, HDIM).astype(F32)
            level = stats[:, 3 * h:3 * h + 1] + stats[:, 3 * h + 1:3 * h + 2] + stats[:, 3 * h + 2:3 * h + 3]
            acc = rm[own, h * GROUPS:(h + 1) * GROUPS, :].reshape(slab, HDIM).astype(F32)
            peak, total, acc = absorb(h, i, 0, first, level, jnp.ones((slab, 1), F32), acc)
            mst[h, slab_rows(i), :] = jnp.broadcast_to(peak, (slab, HDIM))
            lst[h, slab_rows(i), :] = jnp.broadcast_to(total, (slab, HDIM))
            ost[h, slab_rows(i), :] = acc
            return carry

        lax.fori_loop(0, n // block, stage_one, 0)

    count = n * GROUPS
    r = lax.broadcasted_iota(jnp.int32, (count, count), 0)
    k = lax.broadcasted_iota(jnp.int32, (count, count), 1)
    swap = jnp.where(k == (lax.rem(r, n) * GROUPS + r // n), 1.0, 0.0).astype(BF16)
    at_rows = pl.ds(pl.multiple_of(z * n, n), n)
    width = HERE * GROUPS * HDIM
    cut = width // PIECES
    per_head = PIECES // HERE

    def part(core, b, u):
        return att.at[core, pl.ds(pl.multiple_of(b * n, n), n), u * cut:(u + 1) * cut]

    def goes(t, d, u):
        return t < half - 1 or (t == half - 1 and u % 2 == d)

    def ring_block(t, d):
        return lax.rem(z + (chips - 1 - t if d == 0 else 1 + t), chips)

    def along(t, d, u, b):
        ref = part(c, b, u)
        return remote(ref, ref, ag_s.at[d, t, u], ag_r.at[d, t, u], ways[d])

    def across(core, t, d, u, b):
        ref = part(core, b, u)
        return remote(ref, ref, sib_s.at[d, t, u], sib_r.at[d, t, u], sibling)

    def own_across(core, u):
        ref = part(core, z, u)
        return remote(ref, ref, own_sem.at[0, u], own_sem.at[1, u], sibling)

    arrive_all((2, 3), first, n)
    for h in range(HERE):

        def stage_two(i, carry, h=h):
            peak = mst[h, slab_rows(i), 0:1]
            total = lst[h, slab_rows(i), 0:1]
            peak, total, acc = absorb(h, i, first, n, peak, total, ost[h, slab_rows(i), :])
            obuf[h, slab_rows(i), :] = (acc / total).astype(BF16)
            return carry

        lax.fori_loop(0, n // block, stage_two, 0)
        swapped = jnp.dot(swap, obuf[h], preferred_element_type=F32).astype(BF16)
        for g in range(GROUPS):
            begin = (h * GROUPS + g) * HDIM
            att[c, at_rows, begin:begin + HDIM] = swapped[g * n:(g + 1) * n, :]
        for u in range(h * per_head, (h + 1) * per_head):
            for d in range(2):
                if goes(0, d, u):
                    start(along(0, d, u, z))
        for u in range(h * per_head, (h + 1) * per_head):
            start(own_across(c, u))

    fetch_wo.wait()
    projected = jnp.zeros((rows_all, features), F32)

    def project(acc, core, u):
        lanes = slice(u * cut, (u + 1) * cut)
        return acc + jnp.dot(att[core, :, lanes], wov[core, lanes, :], preferred_element_type=F32)

    for t in range(half):
        for u in range(PIECES):
            for d in range(2):
                if not goes(t, d, u):
                    continue
                b = ring_block(t, d)
                along(t, d, u, b).wait_recv()
                if goes(t + 1, d, u):
                    start(along(t + 1, d, u, b))
                start(across(c, t, d, u, b))
            if t == half - 1:
                projected = project(projected, c, u)
    for u in range(PIECES):
        own_across(other, u).wait_recv()
        for t in range(half):
            for d in range(2):
                if goes(t, d, u):
                    across(other, t, d, u, ring_block(t, d)).wait_recv()
        projected = project(projected, other, u)

    mixed[...] = projected.astype(BF16)
    stream = res[...].astype(F32) + projected
    y[...] = (stream * gain[...]).astype(BF16)
    xs[...] = (
        jnp.dot(pick[...].reshape(e * unit, rows_all), y[...], preferred_element_type=F32)
        .astype(BF16)
        .reshape(e, unit, features)
    )

    shift = each * (col // each)

    def target_of(k, i):
        return each * lax.rem(col // each + chips + chips - k, chips) + i

    def slot_at(k):
        return k * each + lax.rem(col, each)

    chunks = []
    for t in range(half):
        for d in range(2):
            if t < half - 1 or d == 0:
                chunks.append(ring_block(t, d))
    chunks.append(z)
    for k in chunks:
        for i in range(each):
            to = target_of(k, i)

            @pl.when(to != col)
            def _(k=k, to=to):
                remote(xs.at[to], xr.at[slot_at(k)], x_s.at[to], x_r.at[slot_at(k)], {"expert": to}).start()

            @pl.when(to == col)
            def _(k=k, to=to):
                xr[slot_at(k)] = xs[to]

    def wait_rows(k):
        for i in range(each):
            b = k * each + i
            src = lax.rem(b + shift, e)

            @pl.when(src != col)
            def _(b=b, src=src):
                remote(xs.at[0], xr.at[b], x_s.at[0], x_r.at[b], {"expert": src}).wait_recv()

    eye = lax.broadcasted_iota(jnp.int32, square, 0) == lax.broadcasted_iota(jnp.int32, square, 1)
    column = jnp.sum(stream * stream, axis=1, keepdims=True)
    flat = jnp.sum(jnp.where(eye, column, 0.0), axis=0, keepdims=True)
    sqs[...] = jnp.broadcast_to(flat, sqs.shape)
    for o in range(1, n):
        start(remote(sqs, sqr.at[o], sq_ss.at[o], sq_rs.at[o], {"sample": lax.rem(me + o, n)}))

    quarter = pown.shape[3] // 2
    ff = 4 * quarter
    fetch_wg.wait()

    def chunk(d, t):
        return lax.rem(z + (chips + chips - 1 - t if d == 0 else 1 + t), chips)

    def partial(gq, dst, d, k):
        own = pl.ds(k * each, each)
        for side in range(2):
            lanes = pl.ds(pl.multiple_of(side * ff + gq * quarter, 128), quarter)
            tiles = {}
            for j, (low, high) in enumerate(spans()):
                lhs = xr[own, low:high, :].reshape(each * (high - low), features)
                got = jnp.dot(lhs, wg[j, :, lanes], preferred_element_type=F32)
                got = got.reshape(each, high - low, quarter)
                for tile in range(low // TILE, high // TILE):
                    piece = got[:, tile * TILE - low:(tile + 1) * TILE - low, :]
                    tiles.setdefault(tile, []).append((j, piece))
            for tile, parts in tiles.items():
                dst[d, own, tile * TILE:(tile + 1) * TILE, side * quarter:(side + 1) * quarter] = (
                    merge_tile(tile, parts).astype(BF16)
                )

    def pair(d, t):
        own = pl.ds(chunk(d, t) * each, each)
        return remote(psib.at[d, own], rsib.at[d, own], ps_s.at[d, t], ps_r.at[d, t], sibling)

    def hop(d, t, u):
        b = chunk(d, t) * each + u
        return remote(pown.at[d, b], rr.at[d, t, u], rs_s.at[d, t, u], rs_r.at[d, t, u], ways[d])

    def prepare(t):
        for d in range(2):
            partial(2 * other + d, psib, d, chunk(d, t))
            pair(d, t).start()
        for d in range(2):
            partial(2 * c + d, pown, d, chunk(d, t))

    def norm_factor():
        squares = sqs[...]
        for o in range(1, n):
            remote(
                sqs, sqr.at[o], sq_ss.at[o], sq_rs.at[o], {"sample": lax.rem(me + n - o, n)}
            ).wait_recv()
            squares = squares + sqr[o]
        factor = lax.rsqrt(squares / (features * n) + EPSILON)[0:1, :]
        for i in range(each):
            to = target_of(z, i)
            values = jnp.sum(pick[to].astype(F32) * factor, axis=1, keepdims=True)
            fsend[i] = jnp.broadcast_to(values, fsend.shape[1:])

            @pl.when(to != col)
            def _(i=i, to=to):
                place_at = lax.rem(col, each)
                remote(fsend.at[i], frecv.at[place_at], f_s.at[i], f_r.at[place_at], {"expert": to}).start()

            @pl.when(to == col)
            def _(i=i):
                frecv[lax.rem(col, each)] = fsend[i]

    def ring(t, carry):
        @pl.when(t < half)
        def _():
            wait_rows(chunk(0, t))

        @pl.when(t < half - 1)
        def _():
            wait_rows(chunk(1, t))

        prepare(t)
        for d in range(2):
            pair(d, t).wait_recv()
        for u in range(each):
            for d in range(2):
                b = chunk(d, t) * each + u

                @pl.when(t == 0)
                def _(d=d, b=b):
                    pown[d, b] = (pown[d, b].astype(F32) + rsib[d, b].astype(F32)).astype(BF16)

                @pl.when(t > 0)
                def _(d=d, b=b, u=u):
                    hop(d, t - 1, u).wait_recv()
                    value = pown[d, b].astype(F32) + rsib[d, b].astype(F32) + rr[d, t - 1, u].astype(F32)
                    pown[d, b] = value.astype(BF16)

                hop(d, t, u).start()

        @pl.when(t == 1)
        def _():
            norm_factor()

        return carry

    lax.fori_loop(0, chips - 1, ring, 0)
    wait_rows(z)
    prepare(chips - 1)
    for i in range(each):
        src = lax.rem(z * each + i + shift, e)

        @pl.when(src != col)
        def _(i=i, src=src):
            remote(fsend.at[0], frecv.at[i], f_s.at[0], f_r.at[i], {"expert": src}).wait_recv()

    for d in range(2):
        pair(d, chips - 1).wait_recv()

    def spread(d, t, u, b):
        return remote(act.at[c, b], act.at[c, b], aa_s.at[d, t, u], aa_r.at[d, t, u], ways[d])

    def hand(core, d, t, u, b):
        return remote(act.at[core, b], act.at[core, b], fw_s.at[d, t, u], fw_r.at[d, t, u], sibling)

    def own_hand(core, u):
        b = z * each + u
        return remote(act.at[core, b], act.at[core, b], me_sem.at[0, u], me_sem.at[1, u], sibling)

    for u in range(each):
        b = z * each + u
        factor = frecv[u][:, 0:1]
        for d in range(2):
            hop(d, chips - 2, u).wait_recv()
            value = pown[d, b].astype(F32) + rsib[d, b].astype(F32) + rr[d, chips - 2, u].astype(F32)
            value = value * factor
            gate = value[:, :quarter]
            act[c, b, :, d * quarter:(d + 1) * quarter] = (
                gate / (1.0 + jnp.exp(-gate)) * value[:, quarter:]
            ).astype(BF16)
        for d in range(2):
            if goes(0, d, u):
                start(spread(d, 0, u, b))
        start(own_hand(c, u))
    fetch_wd.wait()

    def finish(slots):
        tiles = {}
        count = len(slots)
        for j, (low, high) in enumerate(spans()):
            got = None
            for core in range(2):
                lhs = jnp.concatenate([act[core, b, low:high, :] for b in slots], axis=0)
                depth = slice(core * 2 * quarter, (core + 1) * 2 * quarter)
                term = jnp.dot(lhs, wd[j, depth, :], preferred_element_type=F32)
                got = term if got is None else got + term
            got = got.reshape(count, high - low, got.shape[1])
            for tile in range(low // TILE, high // TILE):
                piece = got[:, tile * TILE - low:(tile + 1) * TILE - low, :]
                tiles.setdefault(tile, []).append((j, piece))
        done = {tile: merge_tile(tile, parts).astype(BF16) for tile, parts in tiles.items()}
        for i, b in enumerate(slots):
            for tile, value in done.items():
                osend[b, tile * TILE:(tile + 1) * TILE, :] = value[i]
            target = lax.rem(b + shift, e)

            @pl.when(target != col)
            def _(b=b, target=target):
                remote(osend.at[b], oret.at[col], o_s.at[b], o_r.at[col], {"expert": target}).start()

            @pl.when(target == col)
            def _(b=b):
                oret[col] = osend[b]

    def complete(pending):
        for b, copy in pending:
            copy.wait_recv()
        finish([b for b, copy in pending])

    pending = [(z * each + u, own_hand(other, u)) for u in range(each)]
    for t in range(half):
        if t == half - 1:
            complete(pending)
            pending = []
        fresh = []
        for u in range(each):
            for d in range(2):
                if not goes(t, d, u):
                    continue
                b = ring_block(t, d) * each + u
                spread(d, t, u, b).wait_recv()
                if goes(t + 1, d, u):
                    start(spread(d, t + 1, u, b))
                start(hand(c, d, t, u, b))
                fresh.append((b, hand(other, d, t, u, b)))
        if pending:
            complete(pending)
        pending = fresh
    complete(pending)

    def wait_return(o, carry):
        src = lax.rem(col + o, e)
        remote(osend.at[0], oret.at[src], o_s.at[0], o_r.at[src], {"expert": src}).wait_recv()
        return carry

    lax.fori_loop(1, e, wait_return, 0)
    returned = oret[...].reshape(e * unit, out.shape[1])
    total = jnp.dot(chi[...], returned, preferred_element_type=F32)
    total = total + jnp.dot(clo[...], returned, preferred_element_type=F32)
    out[...] = total.astype(BF16)

    for copy in sent:
        copy.wait_send()

    def drain(t, carry):
        for d in range(2):
            pair(d, t).wait_send()

            @pl.when(t < chips - 1)
            def _(d=d):
                for u in range(each):
                    hop(d, t, u).wait_send()

        return carry

    lax.fori_loop(0, chips, drain, 0)

    def drain_out(b, carry):
        target = lax.rem(b + shift, e)

        @pl.when(target != col)
        def _():
            remote(osend.at[b], oret.at[col], o_s.at[b], o_r.at[col], {"expert": target}).wait_send()

        @pl.when(b != col)
        def _():
            remote(xs.at[b], xr.at[0], x_s.at[b], x_r.at[0], {"expert": b}).wait_send()

        return carry

    lax.fori_loop(0, e, drain_out, 0)
    for i in range(each):
        to = target_of(z, i)

        @pl.when(to != col)
        def _(i=i, to=to):
            remote(fsend.at[i], frecv.at[0], f_s.at[i], f_r.at[0], {"expert": to}).wait_send()


def on_device(
    n, e, queries, prompt_kv, gen_kv, gen_lengths, out_proj, residual, norm_gain,
    w_gate_up, w_down, routes, route_probs,
):
    prompts = queries.shape[0]
    rows = prompts * n
    features = residual.shape[2]
    out_features = w_down.shape[2]
    chips = n // 2
    half = chips // 2
    each = e // chips
    unit = -(-EXP_COL * CAP // TILE) * TILE
    heads = queries.shape[2] // HDIM
    width = HERE * GROUPS * HDIM
    wide = HERE * HDIM
    tokens, gen = prompt_kv.shape[1], gen_kv.shape[2]
    quarter = w_gate_up.shape[2] // 8
    table = 128
    hbm = pl.BlockSpec(memory_space=pltpu.HBM)
    vmem = pl.BlockSpec(memory_space=pltpu.VMEM)
    dma = pltpu.SemaphoreType.DMA
    buf = pltpu.VMEM
    lens = jnp.broadcast_to(gen_lengths.astype(F32)[:, :, None], (prompts, 1, HDIM))
    mixed, expert_out = pl.pallas_call(
        functools.partial(kernel, n, e),
        out_shape=(
            jax.ShapeDtypeStruct((rows, features), BF16),
            jax.ShapeDtypeStruct((rows, out_features), BF16),
        ),
        in_specs=[vmem, vmem, hbm, hbm, hbm, vmem, vmem, vmem, vmem, hbm, hbm],
        out_specs=(vmem, vmem),
        scratch_shapes=[
            buf(prompt_kv.shape, BF16),
            buf((prompts, gen, gen_kv.shape[3]), BF16),
            buf((prompts, 2, (HERE + 1) * GROUPS, HDIM), BF16),
            buf((n, HERE * GROUPS, HDIM), BF16),
            buf((n, (HERE + 1) * GROUPS, HDIM), BF16),
            buf((n, tokens, wide), BF16),
            buf((n, tokens, wide), BF16),
            buf((2, width, features), BF16),
            buf(w_gate_up.shape, BF16),
            buf(w_down.shape, BF16),
            buf((HERE, n * GROUPS, HDIM), F32),
            buf((HERE, n * GROUPS, HDIM), F32),
            buf((HERE, n * GROUPS, HDIM), F32),
            buf((HERE, n * GROUPS, HDIM), BF16),
            buf((2, rows, width), BF16),
            buf((8, rows), F32),
            buf((n, 8, rows), F32),
            buf((rows, table), BF16),
            buf((e, unit, rows), BF16),
            buf((rows, e * unit), BF16),
            buf((rows, e * unit), BF16),
            buf((rows, features), BF16),
            buf((e, unit, features), BF16),
            buf((e, unit, features), BF16),
            buf((2, e, unit, 2 * quarter), BF16),
            buf((2, e, unit, 2 * quarter), BF16),
            buf((2, e, unit, 2 * quarter), BF16),
            buf((2, chips - 1, each, unit, 2 * quarter), BF16),
            buf((2, e, unit, 2 * quarter), BF16),
            buf((e, unit, out_features), BF16),
            buf((e, unit, out_features), BF16),
            buf((each, unit, HDIM), F32),
            buf((each, unit, HDIM), F32),
            dma((7,)),
            dma((4, n)),
            dma((4, n)),
            dma((2, half, PIECES)),
            dma((2, half, PIECES)),
            dma((2, half, PIECES)),
            dma((2, half, PIECES)),
            dma((2, PIECES)),
            dma((n,)),
            dma((n,)),
            dma((e,)),
            dma((e,)),
            dma((2, chips)),
            dma((2, chips)),
            dma((2, chips - 1, each)),
            dma((2, chips - 1, each)),
            dma((2, half, each)),
            dma((2, half, each)),
            dma((2, half, each)),
            dma((2, half, each)),
            dma((2, each)),
            dma((e,)),
            dma((e,)),
            dma((each,)),
            dma((each,)),
        ],
        compiler_params=pltpu.CompilerParams(
            collective_id=0, has_side_effects=True, vmem_limit_bytes=53 << 20
        ),
        name="decode_step",
    )(
        queries.reshape(prompts, heads, HDIM),
        lens,
        prompt_kv,
        gen_kv.reshape(prompts, gen, gen_kv.shape[3]),
        out_proj.reshape(2, width, features),
        residual.reshape(rows, features),
        norm_gain.reshape(1, features),
        jnp.swapaxes(routes, 1, 2),
        jnp.swapaxes(route_probs, 1, 2),
        w_gate_up,
        w_down,
    )
    shape = (prompts, n, features)
    return (mixed.reshape(shape), expert_out.reshape(shape))


def solution(mesh):
    placed = (
        P("expert", "sample", None),
        P("expert", "sample", None),
        P("expert", "sample", None, None),
        P("expert", "sample"),
        P(None, "sample"),
        P("expert", None, "sample"),
        P("sample"),
        P("expert", "sample", None),
        P("expert", None, "sample"),
        P("expert", None, None),
        P("expert", None, None),
    )
    return jax.shard_map(
        functools.partial(on_device, mesh.shape["sample"], mesh.shape["expert"]),
        mesh=mesh,
        in_specs=placed,
        out_specs=(P("expert", None, "sample"), P("expert", None, "sample")),
        check_vma=False,
    )
```

time: 453 us -> 150 us (0.33)
  waiting for transfers between devices: 271 us -> 0 us
  Pallas kernels: 0 us -> 142 us
  local copies, waits for them, and re-layouts: 63.1 us -> 6.33 us
  blocking collectives: 42.2 us -> 0 us
  matrix products: 35.7 us -> 0 us
  other arithmetic: 18.1 us -> 0.66 us
  between operations: 14 us -> 0.65 us
  starting transfers between devices: 6.7 us -> 0 us
    pallas_call x0 -> x1, Pallas kernels: none -> 142 us  [on_device(): pl.pallas_call(functools.partial(kernel, n, e), out_shape=(jax.ShapeDtype...]
    psum x1 -> x0, waiting for transfers between devices: 134 us -> none  [on_device(): lax.psum(partial_sums.astype(jnp.bfloat16), 'sample').astype(jnp.float32)]
    all_gather x2 -> x0, waiting for transfers between devices: 127 us -> none  [the longest x1 96.6 us: on_device(): lax.all_gather(prompt_kv, 'sample', axis=1, tiled=True)]
    dot_general x7 -> x0, matrix products: 35.7 us -> none  [the longest x2 9.46 us: absorb(): jnp.einsum('brhgn,bnhd->brhgd', weights, value_rows.astype(jnp.float32),...]
    psum x1 -> x0, blocking collectives: 23.7 us -> none  [on_device(): squares = lax.psum(jnp.sum(stream * stream, axis=-1), 'sample')]
    unnamed x21 -> x13, local copies, waits for them, and re-layouts: 29.3 us -> 6.26 us
    all_to_all x1 -> x0, blocking collectives: 18.6 us -> none  [on_device(): lax.all_to_all(outgoing, 'expert', split_axis=0, concat_axis=0, tiled=True)]
    convert_element_type x2 -> x0, other arithmetic: 12.5 us -> none  [the longest x1 12.4 us: on_device(): lax.psum(partial_sums.astype(jnp.bfloat16), 'sample').astype(jnp.float32)]
  transfers between devices with their start and end apart: 4 -> 0, of which waited for: 4 -> 0; matrix products, arithmetic and copies ran while one was open for 3% -> 0% of each run, Pallas kernels for 0% -> 0%
where the time goes in v2:
time: 150 us; the launch traced here: 149 us
  Pallas kernels  142 us (95%)
  local copies, waits for them, and re-layouts  6.33 us (4%)
    pallas_call x1, Pallas kernels, on_device(): pl.pallas_call(functools.partial(kernel, n, e), out_shape=(jax.ShapeDtype...  142 us
    unnamed x13, local copies, waits for them, and re-layouts  6.26 us

profile of v2, /device:TPU:1, one launch (start us, length us, event | category | flops | bytes accessed | tf_op | source)
XLA Modules:
  0.0 149.2 jit_solution(9325695216167840258)
XLA Ops:
  0.6 0.7 convert_bitcast_fusion
  1.3 0.1 broadcast_in_dim.9.lens
  1.4 0.9 copy.15
  2.3 0.0 copy-start
  2.3 1.0 copy-done
  3.3 0.0 copy-start.1
  3.3 0.8 copy-done.1
  4.2 0.0 copy-start.2
  4.2 0.8 copy-done.2
  4.9 0.0 copy-start.3
  4.9 0.8 copy-done.3
  5.7 0.0 copy-start.4
  5.7 0.7 copy-done.4
  6.4 141.6 %decode_step.1 = (bf16[128,256]{1,0:T(8,128)(2,1)S(1)}, bf16[128,256]{1,0:T(8,128)(2,1)S(1)}) custom-call(bf16[8,64,128]{2,1,0:T(8,128)(2,1)S(1)} %bitcast.16, f32[8,1,128]{2,1,0:T(1,128)S(1)} %broadcast_in_dim.9.lens, bf16[8,64,1024]{2,1,0:T(8,128)(2,1)} %kv.1, bf16[8,32,1024]{2,1,0:T(8,128)(2,1)S(1)} %bitcast.17, bf16[2,4096,256]{2,1,0:T(8,128)(2,1)} %bitcast.24, ...), custom_call_target="tpu_custom_call" | custom-call | tf_op jit(solution)/shard_map/decode_step/pallas_call | solution.py:685
  148.0 0.6 copy.18
  148.6 0.6 copy.19
Async XLA Ops:
  2.3 1.0 copy-start
  3.3 0.8 copy-start.1
  4.2 0.8 copy-start.2
  4.9 0.8 copy-start.3
  5.7 0.7 copy-start.4

commit v3 on v2

--- a/solution.py
+++ b/solution.py
@@ -53,9 +53,9 @@
 
 def kernel(
     n, e,
-    q, lens, kv, gkv, wo, res, gain, ids, probs, wgu, wdn,
+    q_in, lens_in, kv, gkv, wo, res_in, gain_in, ids_in, probs_in, wgu, wdn,
     mixed, out,
-    kvv, gv, gmsg, rq, rm, rk, rv, wov, wg, wd, ost, mst, lst, obuf, att, sqs, sqr,
+    qraw, qwide, q, lens, res, gain, ids, probs, kvv, gv, gmsg, rq, rm, rkv, wov, wg, wd, ost, mst, lst, obuf, att, sqs, sqr,
     place, pick, chi, clo, y, xs, xr, pown, psib, rsib, rr, act, osend, oret, fsend, frecv,
     lsem, ex_s, ex_r, ag_s, ag_r, sib_s, sib_r, own_sem, sq_ss, sq_rs,
     x_s, x_r, ps_s, ps_r, rs_s, rs_r, aa_s, aa_r, fw_s, fw_r, me_sem, o_s, o_r, f_s, f_r,
@@ -85,8 +85,24 @@
         copy.start()
         return copy
 
+    small = [
+        fetch(a, b, 7 + i)
+        for i, (a, b) in enumerate(
+            ((q_in, qraw), (lens_in, lens), (res_in, res), (gain_in, gain), (ids_in, ids), (probs_in, probs))
+        )
+    ]
     fetch_g = fetch(gkv, gv, 1)
-    fetch_kv = fetch(kv, kvv, 2)
+    fetch_kv = []
+    for hp in range(2):
+        for side in range(2):
+            begin = (2 * side + hp) * HERE * HDIM
+            fetch_kv.append(
+                fetch(
+                    kv.at[:, :, begin:begin + HERE * HDIM],
+                    kvv.at[:, hp, :, side * HERE * HDIM:(side + 1) * HERE * HDIM],
+                    13 + 2 * hp + side,
+                )
+            )
 
     barrier = pltpu.get_barrier_semaphore()
 
@@ -101,12 +117,54 @@
     lax.fori_loop(1, n, greet_sample, 0)
     lax.fori_loop(1, e, greet_expert, 0)
 
-    fetch_g.wait()
+    for copy in small:
+        copy.wait()
+    for h in range(q.shape[1]):
+        qwide[:, h, :] = qraw[:, h * HDIM:(h + 1) * HDIM].astype(F32)
+    q[...] = qwide[...].astype(BF16)
     prompts = q.shape[0]
     gen = gv.shape[1]
     scale = HDIM ** (-0.5)
+    for copy in fetch_kv:
+        copy.wait()
+    pl.semaphore_wait(barrier, n - 1 + e - 1)
+
+    order = token_order(chips)
+    where_of = {d: i for i, d in enumerate(order)}
+
+    def q_pair(p, hp):
+        return q.at[p, pl.ds(pl.multiple_of(hp * HERE * GROUPS, HERE * GROUPS), HERE * GROUPS)], rq.at[me]
+
+    def m_pair(p, hp):
+        return gmsg.at[p, hp], rm.at[me]
+
+    def kv_pair(p, hp, slot):
+        return kvv.at[p, hp], rkv.at[slot]
+
+    def exchange(kind, dz, hp):
+        p = lax.rem(z + dz, chips)
+        slot = 2 * where_of[(chips - dz) % chips] + c
+        src, dst = (q_pair(p, hp), m_pair(p, hp), kv_pair(p, hp, slot))[kind]
+        target = {"sample": 2 * p + hp}
+        start(remote(src, dst, ex_s.at[kind, 2 * dz + (hp if dz else 0)], ex_r.at[kind, slot], target))
+
+    early = order[1:half]
+
+    def send_all(kinds, distances):
+        for dz in distances:
+            for hp in range(2):
+                for kind in kinds:
+                    exchange(kind, dz, hp)
+
+    send_all((2,), early)
+    send_all((0,), order[1:])
+    for kind in (0, 2):
+        exchange(kind, 0, other)
+    fetch_g.wait()
     tall = prompts * GROUPS
-    length = jnp.broadcast_to(lens[...], (prompts, GROUPS, HDIM)).reshape(tall, HDIM)[:, 0:1]
+    of_row = lax.broadcasted_iota(jnp.int32, (tall, prompts), 0) // GROUPS
+    is_row = of_row == lax.broadcasted_iota(jnp.int32, (tall, prompts), 1)
+    length = jnp.sum(jnp.where(is_row, lens[...].astype(F32), 0.0), axis=1, keepdims=True)
     lane = lax.broadcasted_iota(jnp.int32, (tall, HDIM), 1)
     for hp in range(2):
         stats = jnp.zeros((tall, HDIM), F32)
@@ -130,47 +188,11 @@
                 level = level - part
                 stats = jnp.where(lane == 3 * hl + k, part, stats)
         gmsg[:, hp, HERE * GROUPS:, :] = stats.astype(BF16).reshape(prompts, GROUPS, HDIM)
-    fetch_kv.wait()
-
-    pl.semaphore_wait(barrier, n - 1 + e - 1)
-
-    order = token_order(chips)
-    where_of = {d: i for i, d in enumerate(order)}
-
-    def q_pair(p, hp):
-        return q.at[p, pl.ds(pl.multiple_of(hp * HERE * GROUPS, HERE * GROUPS), HERE * GROUPS)], rq.at[me]
-
-    def m_pair(p, hp):
-        return gmsg.at[p, hp], rm.at[me]
-
-    def k_pair(p, hp, slot):
-        return kvv.at[p, :, pl.ds(pl.multiple_of(hp * wide, wide), wide)], rk.at[slot]
-
-    def v_pair(p, hp, slot):
-        return kvv.at[p, :, pl.ds(pl.multiple_of((2 + hp) * wide, wide), wide)], rv.at[slot]
-
-    def exchange(kind, dz, hp):
-        p = lax.rem(z + dz, chips)
-        slot = 2 * where_of[(chips - dz) % chips] + c
-        src, dst = (
-            q_pair(p, hp), m_pair(p, hp), k_pair(p, hp, slot), v_pair(p, hp, slot)
-        )[kind]
-        target = {"sample": 2 * p + hp}
-        start(remote(src, dst, ex_s.at[kind, 2 * dz + (hp if dz else 0)], ex_r.at[kind, slot], target))
-
-    for kind in range(2):
-        for dz in order[1:]:
-            for hp in range(2):
-                exchange(kind, dz, hp)
-        exchange(kind, 0, other)
-    exchange(2, 0, other)
-    exchange(3, 0, other)
-    for dz in order[1:]:
-        for hp in range(2):
-            exchange(2, dz, hp)
-            exchange(3, dz, hp)
+    exchange(1, 0, other)
+    send_all((1,), order[1:])
+    send_all((2,), order[half:])
     local = []
-    for kind, (src, dst) in enumerate((q_pair(z, c), m_pair(z, c), k_pair(z, c, c), v_pair(z, c, c))):
+    for kind, (src, dst) in enumerate((q_pair(z, c), m_pair(z, c), kv_pair(z, c, c))):
         local.append(fetch(src, dst, kind))
     fetch_wo = fetch(wo, wov, 4)
     fetch_wg = fetch(wgu, wg, 5)
@@ -236,10 +258,8 @@
             src, dst = q_pair(0, 0)
         elif kind == 1:
             src, dst = m_pair(0, 0)
-        elif kind == 2:
-            src, dst = k_pair(0, 0, slot)
         else:
-            src, dst = v_pair(0, 0, slot)
+            src, dst = kv_pair(0, 0, slot)
         remote(src, dst, ex_s.at[kind, 1], ex_r.at[kind, slot], sibling).wait_recv()
 
     def arrive_all(kinds, low, high):
@@ -250,11 +270,11 @@
 
         lax.fori_loop(low, high, body, 0)
 
-    for kind in range(4):
+    for kind in range(3):
         arrived(kind, other)
     arrive_all((0, 1), 2, n)
     first = n // 2
-    arrive_all((2, 3), 2, first)
+    arrive_all((2,), 2, first)
     block = min(8, n)
     slab = block * GROUPS
 
@@ -262,9 +282,9 @@
         own = pl.ds(i * block, block)
         query = rq[own, h * GROUPS:(h + 1) * GROUPS, :].reshape(slab, HDIM)
         lanes = slice(h * HDIM, (h + 1) * HDIM)
-        count = (high - low) * rk.shape[1]
-        keys = rk[low:high, :, lanes].reshape(count, HDIM)
-        vals = rv[low:high, :, lanes].reshape(count, HDIM)
+        count = (high - low) * rkv.shape[1]
+        keys = rkv[low:high, :, lanes].reshape(count, HDIM)
+        vals = rkv[low:high, :, wide + h * HDIM:wide + (h + 1) * HDIM].reshape(count, HDIM)
         scores = lax.dot_general(query, keys, NT, preferred_element_type=F32) * scale
         peak = jnp.maximum(highest, jnp.max(scores, axis=1, keepdims=True))
         kept = jnp.exp(highest - peak)
@@ -321,7 +341,7 @@
         ref = part(core, z, u)
         return remote(ref, ref, own_sem.at[0, u], own_sem.at[1, u], sibling)
 
-    arrive_all((2, 3), first, n)
+    arrive_all((2,), first, n)
     for h in range(HERE):
 
         def stage_two(i, carry, h=h):
@@ -373,12 +393,6 @@
     mixed[...] = projected.astype(BF16)
     stream = res[...].astype(F32) + projected
     y[...] = (stream * gain[...]).astype(BF16)
-    xs[...] = (
-        jnp.dot(pick[...].reshape(e * unit, rows_all), y[...], preferred_element_type=F32)
-        .astype(BF16)
-        .reshape(e, unit, features)
-    )
-
     shift = each * (col // each)
 
     def target_of(k, i):
@@ -387,15 +401,10 @@
     def slot_at(k):
         return k * each + lax.rem(col, each)
 
-    chunks = []
-    for t in range(half):
-        for d in range(2):
-            if t < half - 1 or d == 0:
-                chunks.append(ring_block(t, d))
-    chunks.append(z)
-    for k in chunks:
+    def send_rows(k):
         for i in range(each):
             to = target_of(k, i)
+            xs[to] = jnp.dot(pick[to], y[...], preferred_element_type=F32).astype(BF16)
 
             @pl.when(to != col)
             def _(k=k, to=to):
@@ -404,6 +413,9 @@
             @pl.when(to == col)
             def _(k=k, to=to):
                 xr[slot_at(k)] = xs[to]
+
+    send_rows(ring_block(0, 0))
+    send_rows(ring_block(0, 1))
 
     def wait_rows(k):
         for i in range(each):
@@ -421,7 +433,7 @@
     for o in range(1, n):
         start(remote(sqs, sqr.at[o], sq_ss.at[o], sq_rs.at[o], {"sample": lax.rem(me + o, n)}))
 
-    quarter = pown.shape[3] // 2
+    quarter = pown.shape[4]
     ff = 4 * quarter
     fetch_wg.wait()
 
@@ -441,17 +453,18 @@
                     piece = got[:, tile * TILE - low:(tile + 1) * TILE - low, :]
                     tiles.setdefault(tile, []).append((j, piece))
             for tile, parts in tiles.items():
-                dst[d, own, tile * TILE:(tile + 1) * TILE, side * quarter:(side + 1) * quarter] = (
-                    merge_tile(tile, parts).astype(BF16)
-                )
+                dst[d, own, side, tile * TILE:(tile + 1) * TILE, :] = merge_tile(tile, parts).astype(BF16)
 
     def pair(d, t):
         own = pl.ds(chunk(d, t) * each, each)
         return remote(psib.at[d, own], rsib.at[d, own], ps_s.at[d, t], ps_r.at[d, t], sibling)
 
-    def hop(d, t, u):
+    def hop(d, t, u, w):
         b = chunk(d, t) * each + u
-        return remote(pown.at[d, b], rr.at[d, t, u], rs_s.at[d, t, u], rs_r.at[d, t, u], ways[d])
+        return remote(pown.at[d, b, w], rr.at[d, t, u, w], rs_s.at[d, t, u, w], rs_r.at[d, t, u, w], ways[d])
+
+    def pair_sum(d, b, w):
+        return pown[d, b, w].astype(F32) + rsib[d, b, w].astype(F32)
 
     def prepare(t):
         for d in range(2):
@@ -490,25 +503,35 @@
         @pl.when(t < half - 1)
         def _():
             wait_rows(chunk(1, t))
+            send_rows(chunk(0, t + 1))
+
+        @pl.when(t < half - 2)
+        def _():
+            send_rows(chunk(1, t + 1))
+
+        @pl.when(t == half)
+        def _():
+            send_rows(z)
 
         prepare(t)
         for d in range(2):
             pair(d, t).wait_recv()
         for u in range(each):
-            for d in range(2):
-                b = chunk(d, t) * each + u
-
-                @pl.when(t == 0)
-                def _(d=d, b=b):
-                    pown[d, b] = (pown[d, b].astype(F32) + rsib[d, b].astype(F32)).astype(BF16)
-
-                @pl.when(t > 0)
-                def _(d=d, b=b, u=u):
-                    hop(d, t - 1, u).wait_recv()
-                    value = pown[d, b].astype(F32) + rsib[d, b].astype(F32) + rr[d, t - 1, u].astype(F32)
-                    pown[d, b] = value.astype(BF16)
-
-                hop(d, t, u).start()
+            for w in range(2):
+                for d in range(2):
+                    b = chunk(d, t) * each + u
+
+                    @pl.when(t == 0)
+                    def _(d=d, b=b, w=w):
+                        pown[d, b, w] = pair_sum(d, b, w).astype(BF16)
+
+                    @pl.when(t > 0)
+                    def _(d=d, b=b, u=u, w=w):
+                        hop(d, t - 1, u, w).wait_recv()
+                        value = pair_sum(d, b, w) + rr[d, t - 1, u, w].astype(F32)
+                        pown[d, b, w] = value.astype(BF16)
+
+                    hop(d, t, u, w).start()
 
         @pl.when(t == 1)
         def _():
@@ -529,31 +552,36 @@
     for d in range(2):
         pair(d, chips - 1).wait_recv()
 
-    def spread(d, t, u, b):
-        return remote(act.at[c, b], act.at[c, b], aa_s.at[d, t, u], aa_r.at[d, t, u], ways[d])
-
-    def hand(core, d, t, u, b):
-        return remote(act.at[core, b], act.at[core, b], fw_s.at[d, t, u], fw_r.at[d, t, u], sibling)
-
-    def own_hand(core, u):
-        b = z * each + u
-        return remote(act.at[core, b], act.at[core, b], me_sem.at[0, u], me_sem.at[1, u], sibling)
+    def act_part(core, b, w):
+        return act.at[core, b, w]
+
+    def spread(d, t, u, w, b):
+        ref = act_part(c, b, w)
+        return remote(ref, ref, aa_s.at[d, t, u, w], aa_r.at[d, t, u, w], ways[d])
+
+    def hand(core, d, t, u, w, b):
+        ref = act_part(core, b, w)
+        return remote(ref, ref, fw_s.at[d, t, u, w], fw_r.at[d, t, u, w], sibling)
+
+    def own_hand(core, u, w):
+        ref = act_part(core, z * each + u, w)
+        return remote(ref, ref, me_sem.at[0, u, w], me_sem.at[1, u, w], sibling)
 
     for u in range(each):
         b = z * each + u
         factor = frecv[u][:, 0:1]
-        for d in range(2):
-            hop(d, chips - 2, u).wait_recv()
-            value = pown[d, b].astype(F32) + rsib[d, b].astype(F32) + rr[d, chips - 2, u].astype(F32)
-            value = value * factor
-            gate = value[:, :quarter]
-            act[c, b, :, d * quarter:(d + 1) * quarter] = (
-                gate / (1.0 + jnp.exp(-gate)) * value[:, quarter:]
-            ).astype(BF16)
-        for d in range(2):
-            if goes(0, d, u):
-                start(spread(d, 0, u, b))
-        start(own_hand(c, u))
+        for part_of in range(2):
+            sums = []
+            for w in range(2):
+                hop(part_of, chips - 2, u, w).wait_recv()
+                value = pair_sum(part_of, b, w) + rr[part_of, chips - 2, u, w].astype(F32)
+                sums.append(value * factor)
+            gate, up = sums
+            act[c, b, part_of] = (gate / (1.0 + jnp.exp(-gate)) * up).astype(BF16)
+            for d in range(2):
+                if goes(0, d, u):
+                    start(spread(d, 0, u, part_of, b))
+            start(own_hand(c, u, part_of))
     fetch_wd.wait()
 
     def finish(slots):
@@ -562,7 +590,10 @@
         for j, (low, high) in enumerate(spans()):
             got = None
             for core in range(2):
-                lhs = jnp.concatenate([act[core, b, low:high, :] for b in slots], axis=0)
+                halves = [
+                    jnp.concatenate([act[core, b, w, low:high, :] for b in slots], axis=0) for w in range(2)
+                ]
+                lhs = jnp.concatenate(halves, axis=1)
                 depth = slice(core * 2 * quarter, (core + 1) * 2 * quarter)
                 term = jnp.dot(lhs, wd[j, depth, :], preferred_element_type=F32)
                 got = term if got is None else got + term
@@ -585,11 +616,12 @@
                 oret[col] = osend[b]
 
     def complete(pending):
-        for b, copy in pending:
-            copy.wait_recv()
-        finish([b for b, copy in pending])
-
-    pending = [(z * each + u, own_hand(other, u)) for u in range(each)]
+        for b, copies in pending:
+            for copy in copies:
+                copy.wait_recv()
+        finish([b for b, copies in pending])
+
+    pending = [(z * each + u, [own_hand(other, u, w) for w in range(2)]) for u in range(each)]
     for t in range(half):
         if t == half - 1:
             complete(pending)
@@ -599,12 +631,18 @@
             for d in range(2):
                 if not goes(t, d, u):
                     continue
-                b = ring_block(t, d) * each + u
-                spread(d, t, u, b).wait_recv()
-                if goes(t + 1, d, u):
-                    start(spread(d, t + 1, u, b))
-                start(hand(c, d, t, u, b))
-                fresh.append((b, hand(other, d, t, u, b)))
+                fresh.append(
+                    (ring_block(t, d) * each + u, [hand(other, d, t, u, w, ring_block(t, d) * each + u) for w in range(2)])
+                )
+            for w in range(2):
+                for d in range(2):
+                    if not goes(t, d, u):
+                        continue
+                    b = ring_block(t, d) * each + u
+                    spread(d, t, u, w, b).wait_recv()
+                    if goes(t + 1, d, u):
+                        start(spread(d, t + 1, u, w, b))
+                    start(hand(c, d, t, u, w, b))
         if pending:
             complete(pending)
         pending = fresh
@@ -631,7 +669,8 @@
             @pl.when(t < chips - 1)
             def _(d=d):
                 for u in range(each):
-                    hop(d, t, u).wait_send()
+                    for w in range(2):
+                        hop(d, t, u, w).wait_send()
 
         return carry
 
@@ -672,6 +711,7 @@
     each = e // chips
     unit = -(-EXP_COL * CAP // TILE) * TILE
     heads = queries.shape[2] // HDIM
+    topk = routes.shape[2]
     width = HERE * GROUPS * HDIM
     wide = HERE * HDIM
     tokens, gen = prompt_kv.shape[1], gen_kv.shape[2]
@@ -681,23 +721,29 @@
     vmem = pl.BlockSpec(memory_space=pltpu.VMEM)
     dma = pltpu.SemaphoreType.DMA
     buf = pltpu.VMEM
-    lens = jnp.broadcast_to(gen_lengths.astype(F32)[:, :, None], (prompts, 1, HDIM))
     mixed, expert_out = pl.pallas_call(
         functools.partial(kernel, n, e),
         out_shape=(
-            jax.ShapeDtypeStruct((rows, features), BF16),
-            jax.ShapeDtypeStruct((rows, out_features), BF16),
+            pltpu.VMEM((rows, features), BF16),
+            pltpu.VMEM((rows, out_features), BF16),
         ),
-        in_specs=[vmem, vmem, hbm, hbm, hbm, vmem, vmem, vmem, vmem, hbm, hbm],
+        in_specs=[hbm] * 11,
         out_specs=(vmem, vmem),
         scratch_shapes=[
-            buf(prompt_kv.shape, BF16),
+            buf((prompts, heads * HDIM), BF16),
+            buf((prompts, heads, HDIM), F32),
+            buf((prompts, heads, HDIM), BF16),
+            buf((1, prompts), jnp.int32),
+            buf((rows, features), BF16),
+            buf((1, features), F32),
+            buf((prompts, topk, n), jnp.int32),
+            buf((prompts, topk, n), F32),
+            buf((prompts, 2, tokens, 2 * wide), BF16),
             buf((prompts, gen, gen_kv.shape[3]), BF16),
             buf((prompts, 2, (HERE + 1) * GROUPS, HDIM), BF16),
             buf((n, HERE * GROUPS, HDIM), BF16),
             buf((n, (HERE + 1) * GROUPS, HDIM), BF16),
-            buf((n, tokens, wide), BF16),
-            buf((n, tokens, wide), BF16),
+            buf((n, tokens, 2 * wide), BF16),
             buf((2, width, features), BF16),
             buf(w_gate_up.shape, BF16),
             buf(w_down.shape, BF16),
@@ -715,18 +761,18 @@
             buf((rows, features), BF16),
             buf((e, unit, features), BF16),
             buf((e, unit, features), BF16),
-            buf((2, e, unit, 2 * quarter), BF16),
-            buf((2, e, unit, 2 * quarter), BF16),
-            buf((2, e, unit, 2 * quarter), BF16),
-            buf((2, chips - 1, each, unit, 2 * quarter), BF16),
-            buf((2, e, unit, 2 * quarter), BF16),
+            buf((2, e, 2, unit, quarter), BF16),
+            buf((2, e, 2, unit, quarter), BF16),
+            buf((2, e, 2, unit, quarter), BF16),
+            buf((2, chips - 1, each, 2, unit, quarter), BF16),
+            buf((2, e, 2, unit, quarter), BF16),
             buf((e, unit, out_features), BF16),
             buf((e, unit, out_features), BF16),
             buf((each, unit, HDIM), F32),
             buf((each, unit, HDIM), F32),
-            dma((7,)),
-            dma((4, n)),
-            dma((4, n)),
+            dma((17,)),
+            dma((3, n)),
+            dma((3, n)),
             dma((2, half, PIECES)),
             dma((2, half, PIECES)),
             dma((2, half, PIECES)),
@@ -738,25 +784,25 @@
             dma((e,)),
             dma((2, chips)),
             dma((2, chips)),
-            dma((2, chips - 1, each)),
-            dma((2, chips - 1, each)),
-            dma((2, half, each)),
-            dma((2, half, each)),
-            dma((2, half, each)),
-            dma((2, half, each)),
-            dma((2, each)),
+            dma((2, chips - 1, each, 2)),
+            dma((2, chips - 1, each, 2)),
+            dma((2, half, each, 2)),
+            dma((2, half, each, 2)),
+            dma((2, half, each, 2)),
+            dma((2, half, each, 2)),
+            dma((2, each, 2)),
             dma((e,)),
             dma((e,)),
             dma((each,)),
             dma((each,)),
         ],
         compiler_params=pltpu.CompilerParams(
-            collective_id=0, has_side_effects=True, vmem_limit_bytes=53 << 20
+            collective_id=0, has_side_effects=True, vmem_limit_bytes=56 << 20
         ),
         name="decode_step",
     )(
-        queries.reshape(prompts, heads, HDIM),
-        lens,
+        queries.reshape(prompts, heads * HDIM),
+        gen_lengths.T,
         prompt_kv,
         gen_kv.reshape(prompts, gen, gen_kv.shape[3]),
         out_proj.reshape(2, width, features),

time: 150 us -> 145 us (0.967)
  local copies, waits for them, and re-layouts: 6.33 us -> 1.26 us
    unnamed x13 -> x2, local copies, waits for them, and re-layouts: 6.26 us -> 1.26 us
    pallas_call x1, Pallas kernels: 142 us -> 143 us  [on_device(): pl.pallas_call(functools.partial(kernel, n, e), out_shape=(pltpu.VMEM((ro...]
where the time goes in v3:
time: 145 us
  Pallas kernels  143 us (99%)
    pallas_call x1, Pallas kernels, on_device(): pl.pallas_call(functools.partial(kernel, n, e), out_shape=(pltpu.VMEM((ro...  143 us

profile of v3, /device:TPU:1, one launch (start us, length us, event | category | flops | bytes accessed | tf_op | source)
XLA Modules:
  0.0 145.0 jit_solution(3737051224739835485)
XLA Ops:
  0.6 143.1 %decode_step.1 = (bf16[128,256]{1,0:T(8,128)(2,1)S(1)}, bf16[128,256]{1,0:T(8,128)(2,1)S(1)}) custom-call(bf16[8,8192]{1,0:T(8,128)(2,1)} %bitcast.14, s32[1,8]{1,0:T(1,128)} %bitcast.19, bf16[8,64,1024]{2,1,0:T(8,128)(2,1)} %kv.1, bf16[8,32,1024]{2,1,0:T(8,128)(2,1)} %bitcast.13, bf16[2,4096,256]{2,1,0:T(8,128)(2,1)} %bitcast.12, ...), custom_call_target="tpu_custom_call" | custom-call | tf_op jit(solution)/shard_map/decode_step/pallas_call | solution.py:724
  143.8 0.6 copy.15
  144.4 0.6 copy.16

commit v4 on v3

--- a/solution.py
+++ b/solution.py
@@ -240,15 +240,19 @@
     pick[...] = jnp.where(seen.reshape(e, unit, rows_all) == slot_of[:, :, :rows_all], 1.0, 0.0).astype(BF16)
     slot_table = jnp.where(on_lane == 0, slot_of, 0.0).astype(BF16).reshape(e * unit, experts)
     first_lane = jnp.where(lane == 0, 1.0, 0.0).astype(BF16)
-    slot_row = lax.dot_general(first_lane, slot_table, NT, preferred_element_type=F32)
-    placed = lax.dot_general(place[...], table, NT, preferred_element_type=F32)
-    chosen = placed == slot_row
-    for k, ref in enumerate((chi, clo)):
+    share_parts = []
+    for k in range(2):
         part_t = share_t.astype(BF16)
         share_t = share_t - part_t.astype(F32)
-        part = lax.dot_general(eye_bf, part_t, NT, preferred_element_type=F32).astype(BF16)
-        spread_part = lax.dot_general(part, table, NT, preferred_element_type=F32)
-        ref[...] = jnp.where(chosen, spread_part, 0.0).astype(BF16)
+        share_parts.append(lax.dot_general(eye_bf, part_t, NT, preferred_element_type=F32).astype(BF16))
+    for p in range(chips):
+        band = slice(p * each * unit, (p + 1) * each * unit)
+        slot_row = lax.dot_general(first_lane, slot_table[band], NT, preferred_element_type=F32)
+        placed = lax.dot_general(place[...], table[band], NT, preferred_element_type=F32)
+        chosen = placed == slot_row
+        for ref, part in zip((chi, clo), share_parts):
+            spread_part = lax.dot_general(part, table[band], NT, preferred_element_type=F32)
+            ref[p] = jnp.where(chosen, spread_part, 0.0).astype(BF16)
 
     for copy in local:
         copy.wait()
@@ -414,8 +418,11 @@
             def _(k=k, to=to):
                 xr[slot_at(k)] = xs[to]
 
-    send_rows(ring_block(0, 0))
-    send_rows(ring_block(0, 1))
+    for t in range(half - 1):
+        for d in range(2):
+            send_rows(ring_block(t, d))
+    send_rows(ring_block(half - 1, 0))
+    send_rows(z)
 
     def wait_rows(k):
         for i in range(each):
@@ -503,15 +510,6 @@
         @pl.when(t < half - 1)
         def _():
             wait_rows(chunk(1, t))
-            send_rows(chunk(0, t + 1))
-
-        @pl.when(t < half - 2)
-        def _():
-            send_rows(chunk(1, t + 1))
-
-        @pl.when(t == half)
-        def _():
-            send_rows(z)
 
         prepare(t)
         for d in range(2):
@@ -537,8 +535,15 @@
         def _():
             norm_factor()
 
+        @pl.when(t == 2)
+        def _():
+            for copy in sent_before:
+                copy.wait_send()
+
         return carry
 
+    sent_before = list(sent)
+    sent.clear()
     lax.fori_loop(0, chips - 1, ring, 0)
     wait_rows(z)
     prepare(chips - 1)
@@ -621,11 +626,60 @@
                 copy.wait_recv()
         finish([b for b, copies in pending])
 
+    def drain(t, carry):
+        for d in range(2):
+            pair(d, t).wait_send()
+
+            @pl.when(t < chips - 1)
+            def _(d=d):
+                for u in range(each):
+                    for w in range(2):
+                        hop(d, t, u, w).wait_send()
+
+        return carry
+
+    def drain_rows(b, carry):
+        @pl.when(b != col)
+        def _():
+            remote(xs.at[b], xr.at[0], x_s.at[b], x_r.at[0], {"expert": b}).wait_send()
+
+        return carry
+
+    def drain_factor():
+        for i in range(each):
+            to = target_of(z, i)
+
+            @pl.when(to != col)
+            def _(i=i, to=to):
+                remote(fsend.at[i], frecv.at[0], f_s.at[i], f_r.at[0], {"expert": to}).wait_send()
+
+    def step_chunks(t):
+        return [ring_block(t, 0), ring_block(t, 1)] if t < half - 1 else [ring_block(t, 0)]
+
+    def combine(total, ks):
+        for k in ks:
+            for i in range(each):
+                src = target_of(k, i)
+
+                @pl.when(src != col)
+                def _(src=src):
+                    remote(osend.at[0], oret.at[src], o_s.at[0], o_r.at[src], {"expert": src}).wait_recv()
+
+            p = lax.rem(col // each + chips + chips - k, chips)
+            back = oret[pl.ds(p * each, each)].reshape(each * unit, out.shape[1])
+            total = total + jnp.dot(chi[p], back, preferred_element_type=F32)
+            total = total + jnp.dot(clo[p], back, preferred_element_type=F32)
+        return total
+
+    total = jnp.zeros(out.shape, F32)
     pending = [(z * each + u, [own_hand(other, u, w) for w in range(2)]) for u in range(each)]
     for t in range(half):
         if t == half - 1:
             complete(pending)
             pending = []
+            total = combine(total, [z])
+            for early_step in range(half - 3):
+                total = combine(total, step_chunks(early_step))
         fresh = []
         for u in range(each):
             for d in range(2):
@@ -645,36 +699,21 @@
                     start(hand(c, d, t, u, w, b))
         if pending:
             complete(pending)
+        if t == 0:
+            lax.fori_loop(0, chips, drain, 0)
+            lax.fori_loop(0, e, drain_rows, 0)
+            drain_factor()
+        if t == half - 1 and half > 2:
+            total = combine(total, step_chunks(half - 3))
         pending = fresh
     complete(pending)
 
-    def wait_return(o, carry):
-        src = lax.rem(col + o, e)
-        remote(osend.at[0], oret.at[src], o_s.at[0], o_r.at[src], {"expert": src}).wait_recv()
-        return carry
-
-    lax.fori_loop(1, e, wait_return, 0)
-    returned = oret[...].reshape(e * unit, out.shape[1])
-    total = jnp.dot(chi[...], returned, preferred_element_type=F32)
-    total = total + jnp.dot(clo[...], returned, preferred_element_type=F32)
+    for t in range(max(half - 2, 0), half):
+        total = combine(total, step_chunks(t))
     out[...] = total.astype(BF16)
 
     for copy in sent:
         copy.wait_send()
-
-    def drain(t, carry):
-        for d in range(2):
-            pair(d, t).wait_send()
-
-            @pl.when(t < chips - 1)
-            def _(d=d):
-                for u in range(each):
-                    for w in range(2):
-                        hop(d, t, u, w).wait_send()
-
-        return carry
-
-    lax.fori_loop(0, chips, drain, 0)
 
     def drain_out(b, carry):
         target = lax.rem(b + shift, e)
@@ -683,19 +722,9 @@
         def _():
             remote(osend.at[b], oret.at[col], o_s.at[b], o_r.at[col], {"expert": target}).wait_send()
 
-        @pl.when(b != col)
-        def _():
-            remote(xs.at[b], xr.at[0], x_s.at[b], x_r.at[0], {"expert": b}).wait_send()
-
         return carry
 
     lax.fori_loop(0, e, drain_out, 0)
-    for i in range(each):
-        to = target_of(z, i)
-
-        @pl.when(to != col)
-        def _(i=i, to=to):
-            remote(fsend.at[i], frecv.at[0], f_s.at[i], f_r.at[0], {"expert": to}).wait_send()
 
 
 def on_device(
@@ -756,8 +785,8 @@
             buf((n, 8, rows), F32),
             buf((rows, table), BF16),
             buf((e, unit, rows), BF16),
-            buf((rows, e * unit), BF16),
-            buf((rows, e * unit), BF16),
+            buf((chips, rows, each * unit), BF16),
+            buf((chips, rows, each * unit), BF16),
             buf((rows, features), BF16),
             buf((e, unit, features), BF16),
             buf((e, unit, features), BF16),

time: 145 us -> 145 us (level); the launches traced: 145 us -> 143 us
  Pallas kernels: 143 us -> 141 us
    pallas_call x1, Pallas kernels: 143 us -> 141 us  [on_device(): pl.pallas_call(functools.partial(kernel, n, e), out_shape=(pltpu.VMEM((ro...]
where the time goes in v4:
time: 145 us; the launch traced here: 143 us
  Pallas kernels  141 us (97%)
    pallas_call x1, Pallas kernels, on_device(): pl.pallas_call(functools.partial(kernel, n, e), out_shape=(pltpu.VMEM((ro...  141 us

profile of v4, /device:TPU:1, one launch (start us, length us, event | category | flops | bytes accessed | tf_op | source)
XLA Modules:
  0.0 143.3 jit_solution(5184635693786047087)
XLA Ops:
  0.6 141.4 %decode_step.1 = (bf16[128,256]{1,0:T(8,128)(2,1)S(1)}, bf16[128,256]{1,0:T(8,128)(2,1)S(1)}) custom-call(bf16[8,8192]{1,0:T(8,128)(2,1)} %bitcast.14, s32[1,8]{1,0:T(1,128)} %bitcast.19, bf16[8,64,1024]{2,1,0:T(8,128)(2,1)} %kv.1, bf16[8,32,1024]{2,1,0:T(8,128)(2,1)} %bitcast.13, bf16[2,4096,256]{2,1,0:T(8,128)(2,1)} %bitcast.12, ...), custom_call_target="tpu_custom_call" | custom-call | tf_op jit(solution)/shard_map/decode_step/pallas_call | solution.py:753
  142.0 0.6 copy.15
  142.7 0.6 copy.16

commit v5 on v4

--- a/solution.py
+++ b/solution.py
@@ -473,11 +473,12 @@
     def pair_sum(d, b, w):
         return pown[d, b, w].astype(F32) + rsib[d, b, w].astype(F32)
 
-    def prepare(t):
-        for d in range(2):
+    def job(i, t):
+        d = i % 2
+        if i < 2:
             partial(2 * other + d, psib, d, chunk(d, t))
             pair(d, t).start()
-        for d in range(2):
+        else:
             partial(2 * c + d, pown, d, chunk(d, t))
 
     def norm_factor():
@@ -503,33 +504,38 @@
                 frecv[lax.rem(col, each)] = fsend[i]
 
     def ring(t, carry):
-        @pl.when(t < half)
-        def _():
-            wait_rows(chunk(0, t))
-
-        @pl.when(t < half - 1)
-        def _():
-            wait_rows(chunk(1, t))
-
-        prepare(t)
         for d in range(2):
             pair(d, t).wait_recv()
-        for u in range(each):
-            for w in range(2):
-                for d in range(2):
-                    b = chunk(d, t) * each + u
-
-                    @pl.when(t == 0)
-                    def _(d=d, b=b, w=w):
-                        pown[d, b, w] = pair_sum(d, b, w).astype(BF16)
-
-                    @pl.when(t > 0)
-                    def _(d=d, b=b, u=u, w=w):
-                        hop(d, t - 1, u, w).wait_recv()
-                        value = pair_sum(d, b, w) + rr[d, t - 1, u, w].astype(F32)
-                        pown[d, b, w] = value.astype(BF16)
-
-                    hop(d, t, u, w).start()
+        for u, w in [(u, w) for u in range(each) for w in range(2)]:
+            for d in range(2):
+                b = chunk(d, t) * each + u
+
+                @pl.when(t == 0)
+                def _(d=d, b=b, w=w):
+                    pown[d, b, w] = pair_sum(d, b, w).astype(BF16)
+
+                @pl.when(t > 0)
+                def _(d=d, b=b, u=u, w=w):
+                    hop(d, t - 1, u, w).wait_recv()
+                    value = pair_sum(d, b, w) + rr[d, t - 1, u, w].astype(F32)
+                    pown[d, b, w] = value.astype(BF16)
+
+                hop(d, t, u, w).start()
+
+        @pl.when(t + 1 < half)
+        def _():
+            wait_rows(chunk(0, t + 1))
+
+        @pl.when(t + 1 < half - 1)
+        def _():
+            wait_rows(chunk(1, t + 1))
+
+        @pl.when(t + 1 == chips - 1)
+        def _():
+            wait_rows(z)
+
+        for i in range(4):
+            job(i, t + 1)
 
         @pl.when(t == 1)
         def _():
@@ -544,9 +550,11 @@
 
     sent_before = list(sent)
     sent.clear()
+    wait_rows(chunk(0, 0))
+    wait_rows(chunk(1, 0))
+    for i in range(4):
+        job(i, 0)
     lax.fori_loop(0, chips - 1, ring, 0)
-    wait_rows(z)
-    prepare(chips - 1)
     for i in range(each):
         src = lax.rem(z * each + i + shift, e)
 

time: 145 us -> 144 us (level)
  no operation moved by 1% of the time
where the time goes in v5:
time: 144 us; the launch traced here: 143 us
  Pallas kernels  141 us (98%)
    pallas_call x1, Pallas kernels, on_device(): pl.pallas_call(functools.partial(kernel, n, e), out_shape=(pltpu.VMEM((ro...  141 us

profile of v5, /device:TPU:1, one launch (start us, length us, event | category | flops | bytes accessed | tf_op | source)
XLA Modules:
  0.0 142.7 jit_solution(9458258663394034893)
XLA Ops:
  0.6 140.8 %decode_step.1 = (bf16[128,256]{1,0:T(8,128)(2,1)S(1)}, bf16[128,256]{1,0:T(8,128)(2,1)S(1)}) custom-call(bf16[8,8192]{1,0:T(8,128)(2,1)} %bitcast.14, s32[1,8]{1,0:T(1,128)} %bitcast.19, bf16[8,64,1024]{2,1,0:T(8,128)(2,1)} %kv.1, bf16[8,32,1024]{2,1,0:T(8,128)(2,1)} %bitcast.13, bf16[2,4096,256]{2,1,0:T(8,128)(2,1)} %bitcast.12, ...), custom_call_target="tpu_custom_call" | custom-call | tf_op jit(solution)/shard_map/decode_step/pallas_call | solution.py:761
  141.5 0.6 copy.15
  142.1 0.6 copy.16
